TPU v7x, 32 devices: a whole 2x2x4 slice. The times are simulated.
32 devices in a mesh: dp: 16 (over z, y, x), head: 2 (over core).
Axes of the slice: x: 2, y: 2, z: 4, core: 2. Of those that a mesh axis runs over, the one named last changes fastest.
Arguments:
- inputs: bfloat16 [16384, 1280], P(('dp', 'head')), may hold values from -6 to 6
- segment_ids: int32 [32, 512], P(('dp', 'head')), may hold values from 0 to 3, never falling along the last dimension, each value on 1 to 256 neighbouring positions
- gain_attn: float32 [1280], replicated, may hold values from 0.1 to 1.9
- w_qkv: bfloat16 [1280, 3840], replicated, may hold values from -0.15625 to 0.15625
- w_out: bfloat16 [1280, 1280], replicated, may hold values from -1 to 1
- gain_mlp: float32 [1280], replicated, may hold values from 0.1 to 1.9
- w_up: bfloat16 [1280, 5120], replicated, may hold values from -0.15625 to 0.15625
- w_down: bfloat16 [5120, 1280], replicated, may hold values from -0.078125 to 0.078125
- gain_final: float32 [1280], replicated, may hold values from 0.1 to 1.9
- head_projection_weight: bfloat16 [1280, 1280], P(None, 'head'), may hold values from -0.15625 to 0.15625
- head_output_bias: float32 [1280], P('head'), may hold values from -5 to 5
- cotangent: bfloat16 [16384, 1280], P('dp', 'head'), may hold values from -6 to 6
Outputs:
- predicted_levels: float32 [16384, 1280], P('dp', 'head')
- entry_sensitivity_matrix: float32 [16384, 1280], P(('dp', 'head'))
- grad_gain_attn: float32 [1280], P(('dp', 'head'))
- grad_qkv: float32 [1280, 3840], P(('dp', 'head'))
- grad_out: float32 [1280, 1280], P(('dp', 'head'))
- grad_gain_mlp: float32 [1280], P(('dp', 'head'))
- grad_up: float32 [1280, 5120], P(('dp', 'head'))
- grad_down: float32 [5120, 1280], P(('dp', 'head'))
- grad_gain_final: float32 [1280], P(('dp', 'head'))
- grad_head: float32 [1280, 1280], P('dp', 'head')
- grad_bias: float32 [1280], P('head')
Inputs may be any that keep to these rules, and one draw needn't show every extreme that they name: `segment_ids`: in each row the series ids never fall; each series spans 1 to 256 tokens, and in every row one spans exactly 256.
All inputs are finite; a program needn't handle non-finite values.
Results may differ from a plain program's by a relative error of at most 0.017.
Values may be sent and summed in bfloat16 or wider, within the bound.
A program may use at most 320 MiB of HBM per device.

v0:
```python
import math

import jax
import jax.numpy as jnp
from jax import lax
from jax.sharding import PartitionSpec as P

HEADS = 16


epsilon = 1e-06


def rms_forward(values, gain):
    inverse = lax.rsqrt(jnp.mean(values * values, axis=-1, keepdims=True) + epsilon)
    return (values * inverse * gain, inverse)


def rms_backward(values, inverse, gain, grad):
    normed = values * inverse
    scaled = grad * gain
    grad_gain = jnp.sum(grad * normed, axis=0)
    grad_values = inverse * (scaled - normed * jnp.mean(scaled * normed, axis=-1, keepdims=True))
    return (grad_values, grad_gain)


def rotary_tables(sequence_span, hdim):
    half = hdim // 2
    freq = 10000.0 ** (-jnp.arange(half, dtype=jnp.float32) / half)
    angle = jnp.arange(sequence_span, dtype=jnp.float32)[:, None] * freq[None, :]
    return (jnp.cos(angle)[:, None, :], jnp.sin(angle)[:, None, :])


def rotate(values, cosine, sine):
    half = values.shape[-1] // 2
    first = values[..., :half]
    second = values[..., half:]
    return jnp.concatenate(
        [first * cosine - second * sine, second * cosine + first * sine], axis=-1
    )


def unrotate(grads, cosine, sine):
    half = grads.shape[-1] // 2
    first = grads[..., :half]
    second = grads[..., half:]
    return jnp.concatenate(
        [first * cosine + second * sine, second * cosine - first * sine], axis=-1
    )


def allowed_mask(segs):
    place = jnp.arange(segs.shape[0])
    return (segs[:, None] == segs[None, :]) & (place[:, None] >= place[None, :])


def row_scores(query, key, segs, scale):
    scores = jnp.einsum("qhd,khd->hqk", query, key, preferred_element_type=jnp.float32) * scale
    allowed = allowed_mask(segs)[None]
    return (jnp.where(allowed, scores, -1e30), allowed)


def attend_forward(items, scale):
    query, key, value, segs = items
    scores, allowed = row_scores(query, key, segs, scale)
    peak = jnp.max(scores, axis=-1, keepdims=True)
    expo = jnp.exp(scores - peak)
    overall_number = jnp.sum(expo, axis=-1, keepdims=True)
    probs = (expo / overall_number).astype(jnp.bfloat16)
    attended = jnp.einsum("hqk,khd->qhd", probs, value, preferred_element_type=jnp.float32)
    return (attended.astype(jnp.bfloat16), peak + jnp.log(overall_number))


def attend_backward(items, scale):
    query, key, value, segs, log_total, grad_attended = items
    scores, allowed = row_scores(query, key, segs, scale)
    probs = jnp.where(allowed, jnp.exp(scores - log_total), 0.0)
    grad_value = jnp.einsum(
        "hqk,qhd->khd",
        probs.astype(jnp.bfloat16),
        grad_attended,
        preferred_element_type=jnp.float32,
    )
    grad_probs = jnp.einsum(
        "qhd,khd->hqk", grad_attended, value, preferred_element_type=jnp.float32
    )
    grad_scores = (
        probs * (grad_probs - jnp.sum(grad_probs * probs, axis=-1, keepdims=True))
    ).astype(jnp.bfloat16)
    grad_query = (
        jnp.einsum("hqk,khd->qhd", grad_scores, key, preferred_element_type=jnp.float32) * scale
    )
    grad_key = (
        jnp.einsum("hqk,qhd->khd", grad_scores, query, preferred_element_type=jnp.float32) * scale
    )
    return (grad_query, grad_key, grad_value)


def contract_rows(left, right):
    return lax.dot_general(
        left, right, (((0,), (0,)), ((), ())), preferred_element_type=jnp.float32
    )


def contract_cols(left, right):
    return lax.dot_general(
        left, right, (((1,), (1,)), ((), ())), preferred_element_type=jnp.float32
    )


def per_device(
    inputs,
    segment_ids,
    gain_attn,
    w_qkv,
    w_out,
    gain_mlp,
    w_up,
    w_down,
    gain_final,
    head_projection_weight,
    head_output_bias,
    cotangent,
):
    rows, sequence_span = segment_ids.shape
    width = inputs.shape[1]
    hdim = width // HEADS
    scale = 1.0 / math.sqrt(hdim)
    cosine, sine = rotary_tables(sequence_span, hdim)
    tokens = inputs.astype(jnp.float32)
    normed_one, inverse_one = rms_forward(tokens, gain_attn)
    act_one = normed_one.astype(jnp.bfloat16)
    projected = jnp.dot(act_one, w_qkv, preferred_element_type=jnp.float32).reshape(
        rows, sequence_span, 3, HEADS, hdim
    )
    query = rotate(projected[:, :, 0], cosine, sine).astype(jnp.bfloat16)
    key = rotate(projected[:, :, 1], cosine, sine).astype(jnp.bfloat16)
    value = projected[:, :, 2].astype(jnp.bfloat16)
    attended, log_total = lax.map(
        lambda items: attend_forward(items, scale), (query, key, value, segment_ids)
    )
    mixed = attended.reshape(rows * sequence_span, width)
    resid_two = tokens + jnp.dot(mixed, w_out, preferred_element_type=jnp.float32)
    normed_two, inverse_two = rms_forward(resid_two, gain_mlp)
    act_two = normed_two.astype(jnp.bfloat16)
    hidden_pre = jnp.dot(act_two, w_up, preferred_element_type=jnp.float32)
    hidden = jax.nn.silu(hidden_pre).astype(jnp.bfloat16)
    resid_three = resid_two + jnp.dot(hidden, w_down, preferred_element_type=jnp.float32)
    normed_three, inverse_three = rms_forward(resid_three, gain_final)
    final_hidden = normed_three.astype(jnp.bfloat16)
    collected_rows = lax.all_gather(final_hidden, "head", axis=0, tiled=True)
    predicted_levels = (
        jnp.dot(collected_rows, head_projection_weight, preferred_element_type=jnp.float32)
        + head_output_bias
    )
    grad_final = lax.psum_scatter(
        contract_cols(cotangent, head_projection_weight).astype(jnp.bfloat16),
        "head",
        scatter_dimension=0,
        tiled=True,
    ).astype(jnp.float32)
    head_local = contract_rows(collected_rows, cotangent)
    bias_local = jnp.sum(cotangent, axis=0, dtype=jnp.float32)
    grad_head = lax.psum_scatter(head_local, "dp", scatter_dimension=0, tiled=True)
    grad_bias = lax.psum(bias_local, "dp")
    grad_three, grad_gain_final = rms_backward(resid_three, inverse_three, gain_final, grad_final)
    grad_mlp_out = grad_three.astype(jnp.bfloat16)
    grad_down = contract_rows(hidden, grad_mlp_out)
    grad_hidden = contract_cols(grad_mlp_out, w_down)
    sigmoid = jax.nn.sigmoid(hidden_pre)
    grad_pre = (grad_hidden * sigmoid * (1.0 + hidden_pre * (1.0 - sigmoid))).astype(jnp.bfloat16)
    grad_up = contract_rows(act_two, grad_pre)
    grad_norm_two, grad_gain_mlp = rms_backward(
        resid_two, inverse_two, gain_mlp, contract_cols(grad_pre, w_up)
    )
    grad_two = grad_three + grad_norm_two
    mlp_sums = (
        lax.psum_scatter(grad_up, ("dp", "head"), scatter_dimension=0, tiled=True),
        lax.psum_scatter(grad_down, ("dp", "head"), scatter_dimension=0, tiled=True),
        lax.psum_scatter(grad_gain_mlp, ("dp", "head"), scatter_dimension=0, tiled=True),
        lax.psum_scatter(grad_gain_final, ("dp", "head"), scatter_dimension=0, tiled=True),
    )
    grad_branch = grad_two.astype(jnp.bfloat16)
    grad_out = contract_rows(mixed, grad_branch)
    grad_mixed = (
        contract_cols(grad_branch, w_out)
        .astype(jnp.bfloat16)
        .reshape(rows, sequence_span, HEADS, hdim)
    )
    grad_query, grad_key, grad_value = lax.map(
        lambda items: attend_backward(items, scale),
        (query, key, value, segment_ids, log_total, grad_mixed),
    )
    grad_query = unrotate(grad_query, cosine, sine)
    grad_key = unrotate(grad_key, cosine, sine)
    grad_proj = (
        jnp.stack([grad_query, grad_key, grad_value], axis=2)
        .reshape(rows * sequence_span, 3 * width)
        .astype(jnp.bfloat16)
    )
    grad_qkv = contract_rows(act_one, grad_proj)
    grad_norm_one, grad_gain_attn = rms_backward(
        tokens, inverse_one, gain_attn, contract_cols(grad_proj, w_qkv)
    )
    entry_sensitivity_matrix = grad_two + grad_norm_one
    attn_sums = (
        lax.psum_scatter(grad_qkv, ("dp", "head"), scatter_dimension=0, tiled=True),
        lax.psum_scatter(grad_out, ("dp", "head"), scatter_dimension=0, tiled=True),
        lax.psum_scatter(grad_gain_attn, ("dp", "head"), scatter_dimension=0, tiled=True),
    )
    sum_up, sum_down, sum_gain_mlp, sum_gain_final = mlp_sums
    sum_qkv, sum_out, sum_gain_attn = attn_sums
    return (
        predicted_levels,
        entry_sensitivity_matrix,
        sum_gain_attn,
        sum_qkv,
        sum_out,
        sum_gain_mlp,
        sum_up,
        sum_down,
        sum_gain_final,
        grad_head,
        grad_bias,
    )


def solution(mesh):
    return jax.shard_map(
        per_device,
        mesh=mesh,
        in_specs=(
            P(("dp", "head"), None),
            P(("dp", "head"), None),
            P(),
            P(),
            P(),
            P(),
            P(),
            P(),
            P(),
            P(None, "head"),
            P("head"),
            P("dp", "head"),
        ),
        out_specs=(
            P("dp", "head"),
            P(("dp", "head"), None),
            P(("dp", "head")),
            P(("dp", "head"), None),
            P(("dp", "head"), None),
            P(("dp", "head")),
            P(("dp", "head"), None),
            P(("dp", "head"), None),
            P(("dp", "head")),
            P("dp", "head"),
            P("head"),
        ),
        check_vma=False,
    )
```

profile of v0, /device:TPU:0, one launch (start us, length us, event | category | flops | bytes accessed | tf_op | source)
XLA Modules:
  0.0 1168.5 jit_solution(12490002467414584014)
XLA Ops:
  7.2 5.7 convolution_convert_fusion
  14.7 8.7 fusion.46
  24.4 2.4 copy-done.11
  28.4 8.0 fusion.1
  36.4 9.8 fusion
  46.2 9.1 fusion.24
  57.5 13.4 %fusion.59 = f32[512,5120]{1,0:T(8,128)} fusion(bf16[1280,5120]{1,0:T(8,128)(2,1)} %param.18, f32[512,1280]{1,0:T(8,128)S(1)} %get-tuple-element.92, f32[1280]{0:T(1024)S(1)} %copy-done.37, f32[512]{0:T(512)S(1)} %add_rsqrt_fusion.1), kind=kOutput, calls=%fused_computation.105 | convolution fusion | flops 6712852480 | bytes 26221568 | tf_op jit(solution)/shard_map/dot_general | solution.py:146
  71.0 12.2 %multiply_reduce_fusion.3 = (f32[512]{0:T(512)S(1)}, f32[512,1280]{1,0:T(8,128)}) fusion(f32[512,1280]{1,0:T(8,128)S(1)} %get-tuple-element.92, bf16[5120,1280]{1,0:T(8,128)(2,1)S(1)} %bitcast.76, f32[512,5120]{1,0:T(8,128)} %fusion.59), kind=kOutput, calls=%fused_computation.49 | convolution fusion | flops 6725959168 | bytes 28837888 | tf_op jit(solution)/shard_map/dot_general | solution.py:148
  83.2 3.5 fusion.13
  87.3 16.5 %multiply_convert_fusion.1 = bf16[512,5120]{1,0:T(8,128)(2,1)} fusion(f32[512,5120]{1,0:T(8,128)} %fusion.59, bf16[5120,1280]{1,0:T(8,128)(2,1)} %param.19, bf16[512,1280]{1,0:T(8,128)(2,1)} %reduce-scatter.7.cloned.1.call-done, f32[512,1280]{1,0:T(8,128)} %get-tuple-element.94, f32[512]{0:T(512)} %broadcast_multiply_fusion.2, f32[1280]{0:T(1024)S(1)} %copy-done.30, ...), kind=kOutput, calls=%fused_computation.8 | convolution fusion | flops 6739066880 | bytes 32777216 | tf_op jit(solution)/shard_map/dot_general | solution.py:106
  103.8 15.2 %multiply_reduce_fusion.1 = (f32[1280]{0:T(1024)}, f32[512]{0:T(512)S(1)}, f32[512,1280]{1,0:T(8,128)}) fusion(f32[512,1280]{1,0:T(8,128)} %copy-done.6, f32[512]{0:T(512)S(1)} %add_rsqrt_fusion.1, f32[1280]{0:T(1024)} %param.17, bf16[512,5120]{1,0:T(8,128)(2,1)} %multiply_convert_fusion.1, bf16[1280,5120]{1,0:T(8,128)(2,1)} %param.18), kind=kOutput, calls=%fused_computation.43 | convolution fusion | flops 6714817024 | bytes 23607296 | tf_op jit(solution)/shard_map/dot_general | solution.py:106
  119.0 5.2 multiply_add_fusion
  124.3 14.2 %all-gather.2.cloned.1.call-done = bf16[1024,1280]{1,0:T(8,128)(2,1)} async-done(((bf16[512,1280]{1,0:T(8,128)(2,1)}), bf16[1024,1280]{1,0:T(8,128)(2,1)}) %all-gather.2.cloned.1.call-update) | async-done | bytes 2621456 | tf_op jit(solution)/shard_map/all_gather | solution.py:151
  138.5 6.0 fusion.62
  144.6 6.7 fusion.35
  152.9 4.7 convolution_convert_fusion.1
  159.3 13.6 %multiply_reduce_fusion = (f32[16,512]{1,0:T(8,128)S(1)}, f32[16,512,512]{1,2,0:T(8,128)}) fusion(f32[16,512]{1,0:T(8,128)S(1)} %copy-done.27, f32[16,512,512]{1,2,0:T(8,128)} %get-tuple-element.90, pred[512,512]{0,1:T(8,128)(4,1)S(1)} %fusion.29, bf16[512,16,80]{0,2,1:T(8,128)(2,1)S(1)} %bitcast.72, f32[1,512,3,16,80]{1,4,3,2,0:T(8,128)} %bitcast.71), kind=kOutput, calls=%fused_computation.1 | convolution fusion | flops 696246272 | bytes 36503552 | tf_op jit(solution)/shard_map/while/body/eval_jaxpr/qhd,khd->hqk/dot_general | solution.py:84
  172.9 12.9 %multiply_convert_fusion = bf16[16,512,512]{1,2,0:T(8,128)(2,1)S(1)} fusion(f32[16,512,512]{1,2,0:T(8,128)} %get-tuple-element.97, f32[16,512]{1,0:T(8,128)S(1)} %get-tuple-element.96, f32[16,512]{1,0:T(8,128)S(1)} %copy-done.27, f32[16,512,512]{1,2,0:T(8,128)} %get-tuple-element.90, pred[512,512]{0,1:T(8,128)(4,1)S(1)} %fusion.29), kind=kLoop, calls=%fused_computation | loop fusion | flops 29360128 | bytes 42270720 | tf_op jit(solution)/shard_map/while/body/eval_jaxpr/convert_element_type | solution.py:89
  185.9 2.7 multiply_bitcast_fusion
  192.2 8.3 fusion.25
  203.0 10.0 fusion.44
  214.7 15.9 %fusion.38 = f32[5120,1280]{1,0:T(8,128)} fusion(bf16[512,1280]{1,0:T(8,128)(2,1)} %reduce-scatter.7.cloned.1.call-done, f32[512,1280]{1,0:T(8,128)S(1)} %copy-done.8, f32[512]{0:T(512)S(1)} %copy-done.41, f32[1280]{0:T(1024)S(1)} %copy-done.30, f32[512]{0:T(512)S(1)} %add_rsqrt_fusion, f32[512,5120]{1,0:T(8,128)} %fusion.59), kind=kOutput, calls=%fused_computation.79 | convolution fusion | flops 6728581120 | bytes 40641536 | tf_op jit(solution)/shard_map/dot_general | solution.py:100
  232.3 15.0 %fusion.58 = f32[1280,5120]{1,0:T(8,128)} fusion(bf16[512,5120]{1,0:T(8,128)(2,1)} %multiply_convert_fusion.1, f32[512,1280]{1,0:T(8,128)S(1)} %copy-done.7, f32[1280]{0:T(1024)S(1)} %copy-done.39, f32[512]{0:T(512)S(1)} %add_rsqrt_fusion.1), kind=kOutput, calls=%fused_computation.104 | convolution fusion | flops 6712852480 | bytes 34085888 | tf_op jit(solution)/shard_map/dot_general | solution.py:100
  248.9 42.9 %psum.7 = f32[640]{0:T(1024)} all-reduce(f32[640]{0:T(1024)S(1)} %convert_reduce_fusion), channel_id=1, replica_groups=mesh['dp'=16,'head'=2] {'dp'}, use_global_device_ids=true, to_apply=%region_22.23 | all-reduce | flops 640 | bytes 5120 | tf_op jit(solution)/shard_map/psum | solution.py:165
  291.7 11.8 %fusion.19 = (f32[1280]{0:T(1024)S(1)}, f32[512]{0:T(512)S(1)}, f32[512,1280]{1,0:T(8,128)}) fusion(bf16[512,1280]{1,0:T(8,128)(2,1)} %param.12, f32[512]{0:T(512)S(1)} %copy-done.35, f32[1280]{0:T(1024)S(1)} %copy-done.32, bf16[512,3840]{0,1:T(8,128)(2,1)} %bitcast.68, bf16[1280,3840]{1,0:T(8,128)(2,1)} %param.15), kind=kOutput, calls=%fused_computation.37 | convolution fusion | flops 5037750784 | bytes 17709056 | tf_op jit(solution)/shard_map/dot_general | solution.py:106
  303.6 38.6 %all-reduce.3 = (f32[1280]{0:T(1024)S(1)}, f32[1280]{0:T(1024)S(1)}, f32[1280]{0:T(1024)S(1)}) all-reduce(f32[1280]{0:T(1024)S(1)} %get-tuple-element.56, f32[1280]{0:T(1024)S(1)} %copy-done.36, f32[1280]{0:T(1024)S(1)} %copy-done.29), channel_id=3, replica_groups=mesh['dp'=16,'head'=2] {'dp','head'}, use_global_device_ids=true, to_apply=%region_11.12.clone | all-reduce | flops 3840 | bytes 30720
  343.9 4.4 fusion.18
  348.4 3.7 convolution_add_fusion.1
  352.1 24.2 %reduce-scatter.11.cloned.1.call-done = f32[40,1280]{1,0:T(8,128)} async-done(((f32[1280,1280]{1,0:T(8,128)}), f32[40,1280]{1,0:T(8,128)}) %reduce-scatter.11.cloned.1.call-update) | async-done | bytes 204816 | tf_op jit(solution)/shard_map/reduce_scatter | solution.py:208
  376.3 215.9 %reduce-scatter.9.cloned.1.call-done = f32[40,3840]{1,0:T(8,128)} async-done(((f32[1280,3840]{1,0:T(8,128)}), f32[40,3840]{1,0:T(8,128)}) %reduce-scatter.9.cloned.1.call-update) | async-done | bytes 614416 | tf_op jit(solution)/shard_map/reduce_scatter | solution.py:207
  592.2 280.8 %reduce-scatter.15.cloned.1.call-done = f32[160,1280]{1,0:T(8,128)} async-done(((f32[5120,1280]{1,0:T(8,128)}), f32[160,1280]{1,0:T(8,128)}) %reduce-scatter.15.cloned.1.call-update) | async-done | bytes 819216 | tf_op jit(solution)/shard_map/reduce_scatter | solution.py:179
  873.0 288.2 %reduce-scatter.13.cloned.1.call-done = f32[40,5120]{1,0:T(8,128)} async-done(((f32[1280,5120]{1,0:T(8,128)}), f32[40,5120]{1,0:T(8,128)}) %reduce-scatter.13.cloned.1.call-update) | async-done | bytes 819216 | tf_op jit(solution)/shard_map/reduce_scatter | solution.py:178
  (137 shorter events, 23.1 us)
Async XLA Ops:
  7.2 48.1 %copy-start = (bf16[1280,1280]{1,0:T(8,128)(2,1)S(1)}, bf16[1280,1280]{1,0:T(8,128)(2,1)}, u32[]{:S(2)}) copy-start(bf16[1280,1280]{1,0:T(8,128)(2,1)} %param.16) | copy-start | bytes 9830404
  7.2 76.0 %reduce-scatter.7.cloned.1.call-start = ((), (), s32[]{:S(2)}) async-start(), calls=%async_computation.7 | async-start | bytes 3932160 | tf_op jit(solution)/shard_map/reduce_scatter | solution.py:156
  13.0 125.5 %all-gather.2.cloned.1.call-start = ((), (), s32[]{:S(2)}) async-start(), calls=%async_computation.6 | async-start | bytes 3932160 | tf_op jit(solution)/shard_map/all_gather | solution.py:151
  14.7 8.7 copy-start.34
  28.3 8.0 copy-start.12
  28.3 8.0 copy-start.14
  28.3 8.0 copy-start.16
  28.4 8.0 copy-start.18
  46.2 9.1 copy-start.3
  55.3 15.7 %slice-start = ((s8[13107200]{0:T(1024)(128)(4,1)}), s8[4194304]{0:T(1024)(128)(4,1)S(1)}, s32[]{:S(2)}) async-start(s8[13107200]{0:T(1024)(128)(4,1)} %bitcast.75), calls=%async_computation.13 | async-start | bytes 8388608
  57.5 13.5 %copy-start.6 = (f32[512,1280]{1,0:T(8,128)}, f32[512,1280]{1,0:T(8,128)S(1)}, u32[]{:S(2)}) copy-start(f32[512,1280]{1,0:T(8,128)S(1)} %get-tuple-element.92) | copy-start | bytes 7864324
  57.5 13.5 %slice-start.1 = ((s8[13107200]{0:T(1024)(128)(4,1)}), s8[4194304]{0:T(1024)(128)(4,1)S(1)}, s32[]{:S(2)}) async-start(s8[13107200]{0:T(1024)(128)(4,1)} %bitcast.75), calls=%async_computation.14 | async-start | bytes 8388608
  57.5 13.5 %slice-start.2 = ((s8[13107200]{0:T(1024)(128)(4,1)}), s8[4194304]{0:T(1024)(128)(4,1)S(1)}, s32[]{:S(2)}) async-start(s8[13107200]{0:T(1024)(128)(4,1)} %bitcast.75), calls=%async_computation.15 | async-start | bytes 8388608
  57.5 13.5 %slice-start.3 = ((s8[13107200]{0:T(1024)(128)(4,1)}), s8[524288]{0:T(1024)(128)(4,1)S(1)}, s32[]{:S(2)}) async-start(s8[13107200]{0:T(1024)(128)(4,1)} %bitcast.75), calls=%async_computation.16 | async-start | bytes 1048576
  71.0 12.2 %copy-start.30 = (f32[1280]{0:T(1024)S(1)}, f32[1280]{0:T(1024)}, u32[]{:S(2)}) copy-start(f32[1280]{0:T(1024)} %param.20) | copy-start | bytes 15364
  103.8 15.2 %copy-start.9 = (bf16[512,1280]{1,0:T(8,128)(2,1)S(1)}, bf16[512,1280]{1,0:T(8,128)(2,1)}, u32[]{:S(2)}) copy-start(bf16[512,1280]{1,0:T(8,128)(2,1)} %reduce-scatter.7.cloned.1.call-done) | copy-start | bytes 3932164
  103.8 15.2 %copy-start.38 = (f32[1280]{0:T(1024)S(1)}, f32[1280]{0:T(1024)}, u32[]{:S(2)}) copy-start(f32[1280]{0:T(1024)} %param.17) | copy-start | bytes 15364
  103.8 15.2 %copy-start.40 = (f32[512]{0:T(512)S(1)}, f32[512]{0:T(512)}, u32[]{:S(2)}) copy-start(f32[512]{0:T(512)} %broadcast_multiply_fusion.2) | copy-start | bytes 6148
  124.3 227.8 %reduce-scatter.17.cloned.1.call-start = ((), (), s32[]{:S(2)}) async-start(), calls=%async_computation.12 | async-start | bytes 3481600 | tf_op jit(solution)/shard_map/reduce_scatter | solution.py:164
  144.5 231.7 %reduce-scatter.11.cloned.1.call-start = ((), (), s32[]{:S(2)}) async-start(), calls=%async_computation.9 | async-start | bytes 6758400 | tf_op jit(solution)/shard_map/reduce_scatter | solution.py:208
  151.3 440.9 %reduce-scatter.9.cloned.1.call-start = ((), (), s32[]{:S(2)}) async-start(), calls=%async_computation.8 | async-start | bytes 20275200 | tf_op jit(solution)/shard_map/reduce_scatter | solution.py:207
  159.3 13.6 %copy-start.21 = (bf16[512,1280]{0,1:T(8,128)(2,1)}, bf16[512,1280]{0,1:T(8,128)(2,1)S(1)}, u32[]{:S(2)}) copy-start(bf16[512,1280]{0,1:T(8,128)(2,1)S(1)} %copy.40) | copy-start | bytes 3932164
  172.9 12.9 %copy-start.17 = (bf16[512,16,40]{0,2,1:T(8,128)(2,1)S(1)}, bf16[512,16,40]{0,2,1:T(8,128)(2,1)}, u32[]{:S(2)}) copy-start(bf16[512,16,40]{0,2,1:T(8,128)(2,1)} %copy-done.16) | copy-start | bytes 1966084
  172.9 13.0 %copy-start.19 = (bf16[512,16,40]{0,2,1:T(8,128)(2,1)S(1)}, bf16[512,16,40]{0,2,1:T(8,128)(2,1)}, u32[]{:S(2)}) copy-start(bf16[512,16,40]{0,2,1:T(8,128)(2,1)} %copy-done.18) | copy-start | bytes 1966084
  213.0 660.0 %reduce-scatter.15.cloned.1.call-start = ((), (), s32[]{:S(2)}) async-start(), calls=%async_computation.11 | async-start | bytes 27033600 | tf_op jit(solution)/shard_map/reduce_scatter | solution.py:179
  230.6 930.6 %reduce-scatter.13.cloned.1.call-start = ((), (), s32[]{:S(2)}) async-start(), calls=%async_computation.10 | async-start | bytes 27033600 | tf_op jit(solution)/shard_map/reduce_scatter | solution.py:178
  291.7 11.8 %copy-start.29 = (f32[1280]{0:T(1024)S(1)}, f32[1280]{0:T(1024)}, u32[]{:S(2)}) copy-start(f32[1280]{0:T(1024)} %get-tuple-element.54) | copy-start | bytes 15364
  291.7 11.8 %copy-start.36 = (f32[1280]{0:T(1024)S(1)}, f32[1280]{0:T(1024)}, u32[]{:S(2)}) copy-start(f32[1280]{0:T(1024)} %get-tuple-element.52) | copy-start | bytes 15364
  291.7 52.1 %copy-start.2 = (f32[512,1280]{1,0:T(8,128)S(1)}, f32[512,1280]{1,0:T(8,128)}, u32[]{:S(2)}) copy-start(f32[512,1280]{1,0:T(8,128)} %get-tuple-element.81) | copy-start | bytes 7864324
  343.9 4.5 copy-start.42
  343.9 4.5 copy-start.43
  348.4 812.9 %copy-start.1 = (bf16[1280,1280]{1,0:T(8,128)(2,1)S(1)}, bf16[1280,1280]{1,0:T(8,128)(2,1)}, u32[]{:S(2)}) copy-start(bf16[1280,1280]{1,0:T(8,128)(2,1)} %param.16) | copy-start | bytes 9830404
  (24 other events, 50.0 us)
Sparse Core Ops, SparseCore 0:
  13.1 12.8 reduce-scatter.6
  124.4 14.0 all-gather.1
  144.7 85.9 reduce-scatter.16
  233.5 142.7 reduce-scatter.10
  384.3 207.8 reduce-scatter.8
  595.1 277.8 reduce-scatter.14
  876.0 285.1 reduce-scatter.12
where the time goes:
time: 1180 us; the launch traced here: 1170 us
  waiting for transfers between devices  823 us (70%)
  matrix products  191 us (16%)
  blocking collectives  81.4 us (7%)
  other arithmetic  43 us (4%)
  between operations  15.1 us (1%)
  local copies, waits for them, and re-layouts  14.4 us (1%)
    reduce_scatter x1, waiting for transfers between devices, per_device(): lax.psum_scatter(grad_up, ('dp', 'head'), scatter_dimension=0, tiled=True)  288 us
    reduce_scatter x1, waiting for transfers between devices, per_device(): lax.psum_scatter(grad_down, ('dp', 'head'), scatter_dimension=0, tiled=True)  281 us
    reduce_scatter x1, waiting for transfers between devices, per_device(): lax.psum_scatter(grad_qkv, ('dp', 'head'), scatter_dimension=0, tiled=True)  216 us
    dot_general x5, matrix products, contract_cols(): lax.dot_general(left, right, (((1,), (1,)), ((), ())), preferred_element_...  53.9 us
    dot_general x5, matrix products, contract_rows(): lax.dot_general(left, right, (((0,), (0,)), ((), ())), preferred_element_...  53.6 us
    psum x1, blocking collectives, per_device(): grad_bias = lax.psum(bias_local, 'dp')  42.9 us
    unnamed x1, blocking collectives  38.6 us
    reduce_scatter x1, waiting for transfers between devices, per_device(): lax.psum_scatter(grad_out, ('dp', 'head'), scatter_dimension=0, tiled=True)  24.2 us
  transfers between devices with their start and end apart: 7, of which 5 were waited for; matrix products, arithmetic and copies ran while one was open for 16% of the time, Pallas kernels for 0%

commit v1 on v0

--- a/solution.py
+++ b/solution.py
@@ -6,7 +6,8 @@
 from jax.sharding import PartitionSpec as P
 
 HEADS = 16
-
+F32 = jnp.float32
+BF16 = jnp.bfloat16
 
 epsilon = 1e-06
 
@@ -106,6 +107,100 @@
     return lax.dot_general(
         left, right, (((1,), (1,)), ((), ())), preferred_element_type=jnp.float32
     )
+
+
+def swap_cores(values):
+    return lax.ppermute(values, "head", [(0, 1), (1, 0)])
+
+
+def flip(values, bit):
+    size = lax.axis_size("dp")
+    return lax.ppermute(values, "dp", [(i, i ^ bit) for i in range(size)])
+
+
+def sum_everywhere(values, over_head):
+    size = lax.axis_size("dp")
+    if over_head:
+        values = values + swap_cores(values)
+    bit = 1
+    while bit < size:
+        values = values + flip(values, bit)
+        bit *= 2
+    return values
+
+
+def exchange(values, axis, place, bit):
+    kept = lax.dynamic_index_in_dim(values, place, axis, keepdims=False)
+    sent = lax.dynamic_index_in_dim(values, 1 - place, axis, keepdims=False)
+    return kept.astype(F32) + flip(sent.astype(BF16), bit).astype(F32)
+
+
+def line(values, place, stride):
+    length = values.shape[0]
+    size = lax.axis_size("dp")
+
+    def block(index):
+        return lax.dynamic_index_in_dim(
+            values, jnp.clip(index, 0, length - 1), 0, keepdims=False
+        ).astype(F32)
+
+    up = down = None
+    for step in range(1, length):
+        gap = length - step
+        send_up, send_down = block(place + gap), block(place - gap)
+        if up is not None:
+            send_up, send_down = send_up + up.astype(F32), send_down + down.astype(F32)
+        rises = [(i, i + stride) for i in range(size) if i // stride < step]
+        falls = [(i, i - stride) for i in range(size) if i // stride >= length - step]
+        up = lax.ppermute(send_up.astype(BF16), "dp", rises)
+        down = lax.ppermute(send_down.astype(BF16), "dp", falls)
+    total = block(place)
+    if up is not None:
+        total = total + up.astype(F32) + down.astype(F32)
+    return total
+
+
+def reduce_rows(values):
+    size = lax.axis_size("dp")
+    place = lax.axis_index("dp")
+    xi, yi, zi = place & 1, (place >> 1) & 1, place >> 2
+    rows, columns = values.shape
+    length, block = size // 4, rows // size
+    view = values.reshape(length, 2, 2, block, columns)
+    half = columns // 2
+    first, second = view[..., :half], view[..., half:]
+    first = exchange(first, 2, xi, 1).astype(BF16)
+    second = exchange(second, 1, yi, 2).astype(BF16)
+    first = exchange(first, 1, yi, 2).astype(BF16)
+    second = exchange(second, 1, xi, 1).astype(BF16)
+    return jnp.concatenate([line(first, zi, 4), line(second, zi, 4)], axis=1)
+
+
+def finish(values):
+    core = lax.axis_index("head")
+    half = values.shape[0] // 2
+    kept = lax.dynamic_slice_in_dim(values, core * half, half, 0)
+    sent = lax.dynamic_slice_in_dim(values, (1 - core) * half, half, 0)
+    got = swap_cores(sent)
+    return jnp.concatenate(
+        [jnp.where(core == 0, kept, got), jnp.where(core == 0, got, kept)], axis=1
+    )
+
+
+def half_columns(values, core):
+    half = values.shape[1] // 2
+    return lax.dynamic_slice_in_dim(values, core * half, half, 1)
+
+
+def split_halves(values):
+    core = lax.axis_index("head")
+    kept = half_columns(values, core)
+    got = swap_cores(half_columns(values, 1 - core))
+    return jnp.concatenate([kept, got], axis=0)
+
+
+def both(values):
+    return jnp.concatenate([values, swap_cores(values)], axis=0)
 
 
 def per_device(
@@ -122,14 +217,24 @@
     head_output_bias,
     cotangent,
 ):
+    core = lax.axis_index("head")
+    place = lax.axis_index("dp")
     rows, sequence_span = segment_ids.shape
-    width = inputs.shape[1]
+    count, width = inputs.shape
     hdim = width // HEADS
     scale = 1.0 / math.sqrt(hdim)
+
+    other_rows = lax.dynamic_slice_in_dim(cotangent, (1 - core) * count, count, 0)
+    own_rows = lax.dynamic_slice_in_dim(cotangent, core * count, count, 0)
+    got = swap_cores(contract_cols(other_rows, head_projection_weight).astype(BF16))
+    grad_final = contract_cols(own_rows, head_projection_weight) + got.astype(F32)
+    grad_bias = sum_everywhere(jnp.sum(cotangent, axis=0, dtype=F32), False)
+
     cosine, sine = rotary_tables(sequence_span, hdim)
     tokens = inputs.astype(jnp.float32)
     normed_one, inverse_one = rms_forward(tokens, gain_attn)
     act_one = normed_one.astype(jnp.bfloat16)
+    both_one = both(act_one)
     projected = jnp.dot(act_one, w_qkv, preferred_element_type=jnp.float32).reshape(
         rows, sequence_span, 3, HEADS, hdim
     )
@@ -140,48 +245,47 @@
         lambda items: attend_forward(items, scale), (query, key, value, segment_ids)
     )
     mixed = attended.reshape(rows * sequence_span, width)
+    both_mixed = both(mixed)
     resid_two = tokens + jnp.dot(mixed, w_out, preferred_element_type=jnp.float32)
     normed_two, inverse_two = rms_forward(resid_two, gain_mlp)
     act_two = normed_two.astype(jnp.bfloat16)
+    both_two = both(act_two)
     hidden_pre = jnp.dot(act_two, w_up, preferred_element_type=jnp.float32)
     hidden = jax.nn.silu(hidden_pre).astype(jnp.bfloat16)
+    both_hidden = both(hidden)
     resid_three = resid_two + jnp.dot(hidden, w_down, preferred_element_type=jnp.float32)
     normed_three, inverse_three = rms_forward(resid_three, gain_final)
     final_hidden = normed_three.astype(jnp.bfloat16)
-    collected_rows = lax.all_gather(final_hidden, "head", axis=0, tiled=True)
+    other_hidden = swap_cores(final_hidden)
+    collected_rows = jnp.concatenate(
+        [
+            jnp.where(core == 0, final_hidden, other_hidden),
+            jnp.where(core == 0, other_hidden, final_hidden),
+        ],
+        axis=0,
+    )
     predicted_levels = (
         jnp.dot(collected_rows, head_projection_weight, preferred_element_type=jnp.float32)
         + head_output_bias
     )
-    grad_final = lax.psum_scatter(
-        contract_cols(cotangent, head_projection_weight).astype(jnp.bfloat16),
-        "head",
-        scatter_dimension=0,
-        tiled=True,
-    ).astype(jnp.float32)
-    head_local = contract_rows(collected_rows, cotangent)
-    bias_local = jnp.sum(cotangent, axis=0, dtype=jnp.float32)
-    grad_head = lax.psum_scatter(head_local, "dp", scatter_dimension=0, tiled=True)
-    grad_bias = lax.psum(bias_local, "dp")
+    grad_head = reduce_rows(contract_rows(collected_rows, cotangent).astype(BF16))
     grad_three, grad_gain_final = rms_backward(resid_three, inverse_three, gain_final, grad_final)
     grad_mlp_out = grad_three.astype(jnp.bfloat16)
-    grad_down = contract_rows(hidden, grad_mlp_out)
+    grad_down = finish(
+        reduce_rows(contract_rows(both_hidden, split_halves(grad_mlp_out)).astype(BF16))
+    )
     grad_hidden = contract_cols(grad_mlp_out, w_down)
     sigmoid = jax.nn.sigmoid(hidden_pre)
     grad_pre = (grad_hidden * sigmoid * (1.0 + hidden_pre * (1.0 - sigmoid))).astype(jnp.bfloat16)
-    grad_up = contract_rows(act_two, grad_pre)
+    grad_up = finish(reduce_rows(contract_rows(both_two, split_halves(grad_pre)).astype(BF16)))
     grad_norm_two, grad_gain_mlp = rms_backward(
         resid_two, inverse_two, gain_mlp, contract_cols(grad_pre, w_up)
     )
     grad_two = grad_three + grad_norm_two
-    mlp_sums = (
-        lax.psum_scatter(grad_up, ("dp", "head"), scatter_dimension=0, tiled=True),
-        lax.psum_scatter(grad_down, ("dp", "head"), scatter_dimension=0, tiled=True),
-        lax.psum_scatter(grad_gain_mlp, ("dp", "head"), scatter_dimension=0, tiled=True),
-        lax.psum_scatter(grad_gain_final, ("dp", "head"), scatter_dimension=0, tiled=True),
-    )
     grad_branch = grad_two.astype(jnp.bfloat16)
-    grad_out = contract_rows(mixed, grad_branch)
+    grad_out = finish(
+        reduce_rows(contract_rows(both_mixed, split_halves(grad_branch)).astype(BF16))
+    )
     grad_mixed = (
         contract_cols(grad_branch, w_out)
         .astype(jnp.bfloat16)
@@ -198,28 +302,24 @@
         .reshape(rows * sequence_span, 3 * width)
         .astype(jnp.bfloat16)
     )
-    grad_qkv = contract_rows(act_one, grad_proj)
+    grad_qkv = finish(reduce_rows(contract_rows(both_one, split_halves(grad_proj)).astype(BF16)))
     grad_norm_one, grad_gain_attn = rms_backward(
         tokens, inverse_one, gain_attn, contract_cols(grad_proj, w_qkv)
     )
     entry_sensitivity_matrix = grad_two + grad_norm_one
-    attn_sums = (
-        lax.psum_scatter(grad_qkv, ("dp", "head"), scatter_dimension=0, tiled=True),
-        lax.psum_scatter(grad_out, ("dp", "head"), scatter_dimension=0, tiled=True),
-        lax.psum_scatter(grad_gain_attn, ("dp", "head"), scatter_dimension=0, tiled=True),
-    )
-    sum_up, sum_down, sum_gain_mlp, sum_gain_final = mlp_sums
-    sum_qkv, sum_out, sum_gain_attn = attn_sums
+    gains = sum_everywhere(jnp.stack([grad_gain_attn, grad_gain_mlp, grad_gain_final]), True)
+    share = width // (2 * lax.axis_size("dp"))
+    gains = lax.dynamic_slice_in_dim(gains, (place * 2 + core) * share, share, 1)
     return (
         predicted_levels,
         entry_sensitivity_matrix,
-        sum_gain_attn,
-        sum_qkv,
-        sum_out,
-        sum_gain_mlp,
-        sum_up,
-        sum_down,
-        sum_gain_final,
+        gains[0],
+        grad_qkv,
+        grad_out,
+        gains[1],
+        grad_up,
+        grad_down,
+        gains[2],
         grad_head,
         grad_bias,
     )

time: 1180 us -> 689 us (0.58)
  waiting for transfers between devices: 823 us -> 195 us
  starting transfers between devices: 0.46 us -> 213 us
  blocking collectives: 81.4 us -> 0 us
  other arithmetic: 43 us -> 63 us
    reduce_scatter x6 -> x0, waiting for transfers between devices: 809 us -> none  [the longest x1 288 us: per_device(): lax.psum_scatter(grad_up, ('dp', 'head'), scatter_dimension=0, tiled=True)]
    ppermute x0 -> x103, starting transfers between devices: none -> 213 us  [the longest x30 135 us: line(): up = lax.ppermute(send_up.astype(BF16), 'dp', rises)]
    ppermute x0 -> x103, waiting for transfers between devices: none -> 195 us  [the longest x28 140 us: flip(): return lax.ppermute(values, 'dp', [(i, i ^ bit) for i in range(size)])]
    psum x1 -> x0, blocking collectives: 42.9 us -> none  [per_device(): grad_bias = lax.psum(bias_local, 'dp')]
    unnamed x1 -> x0, blocking collectives: 38.6 us -> none
    dot_general x5, matrix products: 53.6 us -> 33.2 us  [contract_rows(): lax.dot_general(left, right, (((0,), (0,)), ((), ())), preferred_element_...]
    convert_element_type x0 -> x54, other arithmetic: none -> 19.6 us  [the longest x1 6.43 us: per_device(): grad_branch = grad_two.astype(jnp.bfloat16)]
    all_gather x1 -> x0, waiting for transfers between devices: 14.2 us -> none  [per_device(): collected_rows = lax.all_gather(final_hidden, 'head', axis=0, tiled=True)]
  transfers between devices with their start and end apart: 7 -> 103, of which waited for: 5 -> 51; matrix products, arithmetic and copies ran while one was open for 16% -> 38% of each run, Pallas kernels for 0% -> 0%
where the time goes in v1:
time: 689 us; the launch traced here: 679 us
  starting transfers between devices  213 us (31%)
  waiting for transfers between devices  195 us (28%)
  matrix products  180 us (26%)
  other arithmetic  63 us (9%)
  local copies, waits for them, and re-layouts  25.1 us (4%)
    ppermute x28, waiting for transfers between devices, flip(): return lax.ppermute(values, 'dp', [(i, i ^ bit) for i in range(size)])  140 us
    ppermute x30, starting transfers between devices, line(): up = lax.ppermute(send_up.astype(BF16), 'dp', rises)  135 us
    dot_general x6, matrix products, contract_cols(): lax.dot_general(left, right, (((1,), (1,)), ((), ())), preferred_element_...  59.6 us
    ppermute x28, starting transfers between devices, flip(): return lax.ppermute(values, 'dp', [(i, i ^ bit) for i in range(size)])  48.7 us
    dot_general x5, matrix products, contract_rows(): lax.dot_general(left, right, (((0,), (0,)), ((), ())), preferred_element_...  33.2 us
    ppermute x30, waiting for transfers between devices, line(): down = lax.ppermute(send_down.astype(BF16), 'dp', falls)  27.8 us
    ppermute x30, starting transfers between devices, line(): down = lax.ppermute(send_down.astype(BF16), 'dp', falls)  26.6 us
    ppermute x30, waiting for transfers between devices, line(): up = lax.ppermute(send_up.astype(BF16), 'dp', rises)  23.7 us
  transfers between devices with their start and end apart: 103, of which 51 were waited for; matrix products, arithmetic and copies ran while one was open for 38% of the time, Pallas kernels for 0%

profile of v1, /device:TPU:0, one launch (start us, length us, event | category | flops | bytes accessed | tf_op | source)
XLA Modules:
  0.0 678.9 jit_solution(13398202770282865572)
XLA Ops:
  6.6 8.4 %fusion.171 = f32[512,3840]{0,1:T(8,128)S(1)} fusion(bf16[512,1280]{1,0:T(8,128)(2,1)S(1)} %fusion.26, bf16[1280,3840]{1,0:T(8,128)(2,1)} %param.15), kind=kOutput, calls=%fused_computation.408 | convolution fusion | flops 5033164800 | bytes 19005440 | tf_op jit(solution)/shard_map/dot_general | solution.py:238
  19.7 8.1 %fusion.1 = (f32[16,512]{1,0:T(8,128)}, f32[16,512,512]{1,2,0:T(8,128)}) fusion(pred[512,512]{0,1:T(8,128)(4,1)S(1)} %fusion.66, bf16[512,16,40]{0,2,1:T(8,128)(2,1)S(1)} %get-tuple-element.171, bf16[512,16,40]{0,2,1:T(8,128)(2,1)S(1)} %get-tuple-element.172, bf16[512,16,40]{0,2,1:T(8,128)(2,1)S(1)} %get-tuple-element.95, ...), kind=kOutput, calls=%fused_computation.8 | convolution fusion | flops 688906240 | bytes 19693568 | tf_op jit(solution)/shard_map/while/body/eval_jaxpr/qhd,khd->hqk/dot_general | solution.py:59
  27.8 9.8 %fusion = f32[16,512]{1,0:T(8,128)} fusion(f32[16,512,512]{1,2,0:T(8,128)} %get-tuple-element.179, f32[16,512]{1,0:T(8,128)} %get-tuple-element.178, pred[512,512]{0,1:T(8,128)(4,1)S(1)} %fusion.66), kind=kLoop, calls=%fused_computation.6 | loop fusion | flops 16769024 | bytes 17104896 | tf_op jit(solution)/shard_map/while/body/eval_jaxpr/reduce_sum | solution.py:69
  37.6 9.9 %fusion.53 = bf16[16,80,512]{2,1,0:T(8,128)(2,1)} fusion(f32[16,512,512]{1,2,0:T(8,128)} %get-tuple-element.179, f32[16,512]{1,0:T(8,128)} %fusion, f32[16,512]{1,0:T(8,128)} %get-tuple-element.178, pred[512,512]{0,1:T(8,128)(4,1)S(1)} %fusion.66, f32[1,512,3,16,80]{1,4,3,2,0:T(8,128)} %bitcast.404), kind=kOutput, calls=%fused_computation.105 | convolution fusion | flops 692715520 | bytes 19726336 | tf_op jit(solution)/shard_map/while/body/eval_jaxpr/hqk,khd->qhd/dot_general | solution.py:71
  51.5 17.3 %multiply_convert_fusion.2 = (bf16[512,5120]{1,0:T(8,128)(2,1)}, f32[512,5120]{1,0:T(8,128)}) fusion(bf16[512,1280]{1,0:T(8,128)(2,1)S(1)} %multiply_convert_fusion.4, bf16[1280,5120]{1,0:T(8,128)(2,1)} %param.18), kind=kOutput, calls=%fused_computation.14 | convolution fusion | flops 6723993600 | bytes 30146560 | tf_op jit(solution)/shard_map/dot_general | solution.py:253
  72.2 10.6 %multiply_reduce_fusion.5 = (f32[512]{0:T(512)S(1)}, f32[512,1280]{1,0:T(8,128)}) fusion(f32[512,1280]{1,0:T(8,128)S(1)} %get-tuple-element.181, bf16[512,5120]{1,0:T(8,128)(2,1)} %get-tuple-element.182, bf16[5120,1280]{1,0:T(8,128)(2,1)S(1)} %bitcast.421), kind=kOutput, calls=%fused_computation.83 | convolution fusion | flops 6712851968 | bytes 23595008 | tf_op jit(solution)/shard_map/dot_general | solution.py:256
  100.6 5.1 multiply_reduce_fusion.1
  109.7 20.8 %multiply_convert_fusion.1 = bf16[512,5120]{1,0:T(8,128)(2,1)} fusion(f32[512,5120]{1,0:T(8,128)} %get-tuple-element.183, bf16[512,1280]{1,0:T(8,128)(2,1)S(1)} %fusion.164, bf16[5120,1280]{1,0:T(8,128)(2,1)} %param.19), kind=kOutput, calls=%fused_computation.13 | convolution fusion | flops 6734479360 | bytes 30146560 | tf_op jit(solution)/shard_map/dot_general | solution.py:107
  130.5 15.1 %multiply_reduce_fusion.2 = (f32[1280]{0:T(1024)}, f32[512]{0:T(512)S(1)}, f32[512,1280]{1,0:T(8,128)}) fusion(f32[512,1280]{1,0:T(8,128)} %copy-done.2, f32[512]{0:T(512)S(1)} %copy-done.50, f32[1280]{0:T(1024)S(1)} %copy-done.44, bf16[512,5120]{1,0:T(8,128)(2,1)} %multiply_convert_fusion.1, bf16[1280,5120]{1,0:T(8,128)(2,1)} %param.18), kind=kOutput, calls=%fused_computation.74 | convolution fusion | flops 6714817024 | bytes 23607296 | tf_op jit(solution)/shard_map/dot_general | solution.py:107
  145.6 6.4 fusion.165
  157.7 13.6 %multiply_reduce_fusion = (f32[16,512]{1,0:T(8,128)S(1)}, f32[16,512,512]{1,2,0:T(8,128)}) fusion(f32[16,512]{1,0:T(8,128)S(1)} %copy-done.39, f32[16,512,512]{1,2,0:T(8,128)} %get-tuple-element.179, pred[512,512]{0,1:T(8,128)(4,1)S(1)} %fusion.66, bf16[512,16,80]{0,2,1:T(8,128)(2,1)S(1)} %bitcast.413, f32[1,512,3,16,80]{1,4,3,2,0:T(8,128)} %bitcast.405), kind=kOutput, calls=%fused_computation.1 | convolution fusion | flops 696246272 | bytes 36503552 | tf_op jit(solution)/shard_map/while/body/eval_jaxpr/qhd,khd->hqk/dot_general | solution.py:85
  171.3 12.7 %multiply_convert_fusion = bf16[16,512,512]{1,2,0:T(8,128)(2,1)S(1)} fusion(f32[16,512,512]{1,2,0:T(8,128)} %get-tuple-element.189, f32[16,512]{1,0:T(8,128)S(1)} %get-tuple-element.188, f32[16,512]{1,0:T(8,128)S(1)} %copy-done.39, f32[16,512,512]{1,2,0:T(8,128)} %get-tuple-element.179, pred[512,512]{0,1:T(8,128)(4,1)S(1)} %fusion.66), kind=kLoop, calls=%fused_computation | loop fusion | flops 29360128 | bytes 42270720 | tf_op jit(solution)/shard_map/while/body/eval_jaxpr/convert_element_type | solution.py:90
  188.2 8.4 %fusion.54 = bf16[1,512,1,16,80]{1,4,3,2,0:T(8,128)(2,1)S(1)} fusion(bf16[512,16,80]{0,2,1:T(8,128)(2,1)S(1)} %bitcast.414, f32[16,512]{1,0:T(8,128)S(1)} %copy-done.40, f32[16,512,512]{1,2,0:T(8,128)} %get-tuple-element.179, pred[512,512]{0,1:T(8,128)(4,1)S(1)} %fusion.66), kind=kOutput, calls=%fused_computation.106 | convolution fusion | flops 692715520 | bytes 19693568 | tf_op jit(solution)/shard_map/while/body/eval_jaxpr/hqk,qhd->khd/dot_general | solution.py:79
  200.7 11.6 %fusion.31 = (f32[1280]{0:T(1024)S(1)}, f32[512]{0:T(512)S(1)}, f32[512,1280]{1,0:T(8,128)}) fusion(bf16[512,1280]{1,0:T(8,128)(2,1)S(1)} %copy-done.7, f32[512]{0:T(512)S(1)} %copy-done.52, f32[1280]{0:T(1024)S(1)} %copy-done.46, bf16[512,3840]{0,1:T(8,128)(2,1)S(1)} %bitcast.396, bf16[1280,3840]{1,0:T(8,128)(2,1)} %param.15), kind=kOutput, calls=%fused_computation.53 | convolution fusion | flops 5037750784 | bytes 17709056 | tf_op jit(solution)/shard_map/dot_general | solution.py:107
  249.0 5.7 collective-permute-done.83
  258.4 8.7 %collective-permute-done.36 = bf16[4,2,80,320]{3,2,0,1:T(8,128)(2,1)S(1)} collective-permute-done((bf16[4,2,80,320]{3,2,0,1:T(8,128)(2,1)S(1)}, bf16[4,2,80,320]{3,2,0,1:T(8,128)(2,1)S(1)}, u32[]{:S(2)}, u32[]{:S(2)}) %collective-permute-start.36) | collective-permute-done | bytes 409632 | tf_op jit(solution)/shard_map/ppermute | solution.py:118
  270.3 5.5 collective-permute-done.84
  299.6 5.9 convolution_convert_fusion.1
  356.3 19.0 %collective-permute-start.40 = (bf16[80,320]{1,0:T(8,128)(2,1)S(1)}, bf16[80,320]{1,0:T(8,128)(2,1)S(1)}, u32[]{:S(2)}, u32[]{:S(2)}) collective-permute-start(bf16[80,320]{1,0:T(8,128)(2,1)S(1)} %get-tuple-element.161), channel_id=1, source_target_pairs={{0,8},{2,10},{4,12},{6,14},{8,16},{10,18},{12,20},{14,22},{16,24},... | collective-permute-start | bytes 153608 | tf_op jit(solution)/shard_map/ppermute | solution.py:155
  399.9 9.0 %convolution_convert_fusion = bf16[1280,2560]{1,0:T(8,128)(2,1)S(1)} fusion(bf16[512,2560]{1,0:T(8,128)(2,1)} %collective-permute-done.46, bf16[512,2560]{1,0:T(8,128)(2,1)S(1)} %copy-done.25, bf16[512,1280]{1,0:T(8,128)(2,1)S(1)} %collective-permute-done.45, bf16[512,1280]{1,0:T(8,128)(2,1)S(1)} %copy-done.28), kind=kOutput, calls=%fused_computation.7 | convolution fusion | flops 6729891840 | bytes 14417920 | tf_op jit(solution)/shard_map/dot_general | solution.py:101
  410.9 16.1 %collective-permute-done.17 = bf16[4,2,80,960]{3,2,0,1:T(8,128)(2,1)} collective-permute-done((bf16[4,2,80,960]{3,2,0,1:T(8,128)(2,1)S(1)}, bf16[4,2,80,960]{3,2,0,1:T(8,128)(2,1)}, u32[]{:S(2)}, u32[]{:S(2)}) %collective-permute-start.17) | collective-permute-done | bytes 1228832 | tf_op jit(solution)/shard_map/ppermute | solution.py:118
  435.1 9.7 %collective-permute-done.18 = bf16[4,80,960]{2,1,0:T(8,128)(2,1)S(1)} collective-permute-done((bf16[4,80,960]{2,1,0:T(8,128)(2,1)S(1)}, bf16[4,80,960]{2,1,0:T(8,128)(2,1)S(1)}, u32[]{:S(2)}, u32[]{:S(2)}) %collective-permute-start.18) | collective-permute-done | bytes 614432 | tf_op jit(solution)/shard_map/ppermute | solution.py:118
  446.8 28.8 %collective-permute-done.10 = bf16[4,80,960]{2,1,0:T(8,128)(2,1)S(1)} collective-permute-done((bf16[4,80,960]{2,1,0:T(8,128)(2,1)S(1)}, bf16[4,80,960]{2,1,0:T(8,128)(2,1)S(1)}, u32[]{:S(2)}, u32[]{:S(2)}) %collective-permute-start.10) | collective-permute-done | bytes 614432 | tf_op jit(solution)/shard_map/ppermute | solution.py:118
  481.9 11.5 %fusion.9 = bf16[5120,640]{1,0:T(8,128)(2,1)S(1)} fusion(bf16[512,5120]{1,0:T(8,128)(2,1)} %collective-permute-done.64, bf16[512,5120]{1,0:T(8,128)(2,1)} %get-tuple-element.182, bf16[512,640]{1,0:T(8,128)(2,1)} %collective-permute-done.65, bf16[512,640]{1,0:T(8,128)(2,1)S(1)} %copy-done.37), kind=kOutput, calls=%fused_computation.19 | convolution fusion | flops 6737756160 | bytes 18350080 | tf_op jit(solution)/shard_map/dot_general | solution.py:101
  510.5 5.0 collective-permute-start.21
  518.3 12.2 %collective-permute-start.13 = (bf16[80,960]{1,0:T(8,128)(2,1)S(1)}, bf16[80,960]{1,0:T(8,128)(2,1)S(1)}, u32[]{:S(2)}, u32[]{:S(2)}) collective-permute-start(bf16[80,960]{1,0:T(8,128)(2,1)S(1)} %get-tuple-element.147), channel_id=1, source_target_pairs={{0,8},{2,10},{4,12},{6,14},{8,16},{10,18},{12,20},{14,22},{16,24},... | collective-permute-start | bytes 460808 | tf_op jit(solution)/shard_map/ppermute | solution.py:155
  542.7 25.1 %collective-permute-done.56 = bf16[4,80,1280]{2,1,0:T(8,128)(2,1)S(1)} collective-permute-done((bf16[4,80,1280]{2,1,0:T(8,128)(2,1)S(1)}, bf16[4,80,1280]{2,1,0:T(8,128)(2,1)S(1)}, u32[]{:S(2)}, u32[]{:S(2)}) %collective-permute-start.56) | collective-permute-done | bytes 819232 | tf_op jit(solution)/shard_map/ppermute | solution.py:118
  591.5 5.4 collective-permute-start.51
  602.2 5.6 collective-permute-done.62
  621.3 13.8 %collective-permute-done.67 = bf16[4,320,320]{2,1,0:T(8,128)(2,1)S(1)} collective-permute-done((bf16[4,320,320]{2,1,0:T(8,128)(2,1)S(1)}, bf16[4,320,320]{2,1,0:T(8,128)(2,1)S(1)}, u32[]{:S(2)}, u32[]{:S(2)}) %collective-permute-start.67) | collective-permute-done | bytes 819232 | tf_op jit(solution)/shard_map/ppermute | solution.py:118
  657.7 5.2 collective-permute-start.70
  665.6 7.0 %collective-permute-done.81 = bf16[320,320]{1,0:T(8,128)(2,1)S(1)} collective-permute-done((bf16[320,320]{1,0:T(8,128)(2,1)S(1)}, bf16[320,320]{1,0:T(8,128)(2,1)S(1)}, u32[]{:S(2)}, u32[]{:S(2)}) %collective-permute-start.81) | collective-permute-done | bytes 204832 | tf_op jit(solution)/shard_map/ppermute | solution.py:156
  (482 shorter events, 318.5 us)
Async XLA Ops:
  4.8 95.8 %collective-permute-start.1 = (bf16[512,1280]{1,0:T(8,128)(2,1)}, bf16[512,1280]{1,0:T(8,128)(2,1)}, u32[]{:S(2)}, u32[]{:S(2)}) collective-permute-start(bf16[512,1280]{1,0:T(8,128)(2,1)} %convolution_convert_fusion.4), channel_id=1, source_target_pairs={{0,1},{1,0},{2,3},{3,2},{4,5},{5,4},{6,7},{7,6},{8,9},{9,8},{10,11... | collective-permute-start | bytes 3932168 | tf_op jit(solution)/shard_map/ppermute | solution.py:113
  47.5 183.6 %collective-permute-start.26 = (bf16[512,1280]{0,1:T(8,128)(2,1)}, bf16[512,1280]{0,1:T(8,128)(2,1)}, u32[]{:S(2)}, u32[]{:S(2)}) collective-permute-start(bf16[512,1280]{0,1:T(8,128)(2,1)} %bitcast.10), channel_id=1, source_target_pairs={{0,1},{1,0},{2,3},{3,2},{4,5},{5,4},{6,7},{7,6},{8,9},{9,8},{10,11... | collective-permute-start | bytes 3932168 | tf_op jit(solution)/shard_map/ppermute | solution.py:113
  68.8 411.6 %collective-permute-start.64 = (bf16[512,5120]{1,0:T(8,128)(2,1)}, bf16[512,5120]{1,0:T(8,128)(2,1)}, u32[]{:S(2)}, u32[]{:S(2)}) collective-permute-start(bf16[512,5120]{1,0:T(8,128)(2,1)} %get-tuple-element.182), channel_id=1, source_target_pairs={{0,1},{1,0},{2,3},{3,2},{4,5},{5,4},{6,7},{7,6},{8,9},{9,8},{10,11... | collective-permute-start | bytes 15728648 | tf_op jit(solution)/shard_map/ppermute | solution.py:113
  197.8 33.9 %collective-permute-start.27 = (bf16[512,640]{1,0:T(8,128)(2,1)}, bf16[512,640]{1,0:T(8,128)(2,1)}, u32[]{:S(2)}, u32[]{:S(2)}) collective-permute-start(bf16[512,640]{1,0:T(8,128)(2,1)} %get-tuple-element.114), channel_id=1, source_target_pairs={{0,1},{1,0},{2,3},{3,2},{4,5},{5,4},{6,7},{7,6},{8,9},{9,8},{10,11... | collective-permute-start | bytes 1966088 | tf_op jit(solution)/shard_map/ppermute | solution.py:113
  198.4 37.9 %collective-permute-start = (bf16[512,1280]{1,0:T(8,128)(2,1)S(1)}, bf16[512,1280]{1,0:T(8,128)(2,1)}, u32[]{:S(2)}, u32[]{:S(2)}) collective-permute-start(bf16[512,1280]{1,0:T(8,128)(2,1)S(1)} %copy-done.11), channel_id=1, source_target_pairs={{0,1},{1,0},{2,3},{3,2},{4,5},{5,4},{6,7},{7,6},{8,9},{9,8},{10,11... | collective-permute-start | bytes 3932168 | tf_op jit(solution)/shard_map/ppermute | solution.py:113
  230.5 167.6 %collective-permute-start.45 = (bf16[512,1280]{1,0:T(8,128)(2,1)S(1)}, bf16[512,1280]{1,0:T(8,128)(2,1)S(1)}, u32[]{:S(2)}, u32[]{:S(2)}) collective-permute-start(bf16[512,1280]{1,0:T(8,128)(2,1)S(1)} %copy-done.28), channel_id=1, source_target_pairs={{0,1},{1,0},{2,3},{3,2},{4,5},{5,4},{6,7},{7,6},{8,9},{9,8},{10,11... | collective-permute-start | bytes 3932168 | tf_op jit(solution)/shard_map/ppermute | solution.py:113
  231.1 64.3 %collective-permute-start.7 = (bf16[512,1280]{1,0:T(8,128)(2,1)S(1)}, bf16[512,1280]{1,0:T(8,128)(2,1)S(1)}, u32[]{:S(2)}, u32[]{:S(2)}) collective-permute-start(bf16[512,1280]{1,0:T(8,128)(2,1)S(1)} %copy-done.32), channel_id=1, source_target_pairs={{0,1},{1,0},{2,3},{3,2},{4,5},{5,4},{6,7},{7,6},{8,9},{9,8},{10,11... | collective-permute-start | bytes 3932168 | tf_op jit(solution)/shard_map/ppermute | solution.py:113
  267.1 31.8 %collective-permute-start.8 = (bf16[512,1920]{0,1:T(8,128)(2,1)S(1)}, bf16[512,1920]{0,1:T(8,128)(2,1)S(1)}, u32[]{:S(2)}, u32[]{:S(2)}) collective-permute-start(bf16[512,1920]{0,1:T(8,128)(2,1)S(1)} %get-tuple-element.85), channel_id=1, source_target_pairs={{0,1},{1,0},{2,3},{3,2},{4,5},{5,4},{6,7},{7,6},{8,9},{9,8},{10,11... | collective-permute-start | bytes 5898248 | tf_op jit(solution)/shard_map/ppermute | solution.py:113
  295.3 104.6 %collective-permute-start.46 = (bf16[512,2560]{1,0:T(8,128)(2,1)S(1)}, bf16[512,2560]{1,0:T(8,128)(2,1)}, u32[]{:S(2)}, u32[]{:S(2)}) collective-permute-start(bf16[512,2560]{1,0:T(8,128)(2,1)S(1)} %get-tuple-element.77), channel_id=1, source_target_pairs={{0,1},{1,0},{2,3},{3,2},{4,5},{5,4},{6,7},{7,6},{8,9},{9,8},{10,11... | collective-permute-start | bytes 7864328 | tf_op jit(solution)/shard_map/ppermute | solution.py:113
  298.9 28.9 %collective-permute-start.88 = (bf16[80,320]{1,0:T(8,128)(2,1)S(1)}, bf16[80,320]{1,0:T(8,128)(2,1)S(1)}, u32[]{:S(2)}, u32[]{:S(2)}) collective-permute-start(bf16[80,320]{1,0:T(8,128)(2,1)S(1)} %get-tuple-element.156), channel_id=1, source_target_pairs={{24,16},{26,18},{28,20},{30,22},{25,17},{27,19},{29,21},{31,23}} | collective-permute-start | bytes 153608 | tf_op jit(solution)/shard_map/ppermute | solution.py:156
  355.0 20.7 %collective-permute-start.90 = (bf16[80,320]{1,0:T(8,128)(2,1)S(1)}, bf16[80,320]{1,0:T(8,128)(2,1)S(1)}, u32[]{:S(2)}, u32[]{:S(2)}) collective-permute-start(bf16[80,320]{1,0:T(8,128)(2,1)S(1)} %fusion.128), channel_id=1, source_target_pairs={{8,0},{10,2},{12,4},{14,6},{16,8},{18,10},{20,12},{22,14},{24,16},... | collective-permute-start | bytes 153608 | tf_op jit(solution)/shard_map/ppermute | solution.py:156
  356.3 20.9 %collective-permute-start.40 = (bf16[80,320]{1,0:T(8,128)(2,1)S(1)}, bf16[80,320]{1,0:T(8,128)(2,1)S(1)}, u32[]{:S(2)}, u32[]{:S(2)}) collective-permute-start(bf16[80,320]{1,0:T(8,128)(2,1)S(1)} %get-tuple-element.161), channel_id=1, source_target_pairs={{0,8},{2,10},{4,12},{6,14},{8,16},{10,18},{12,20},{14,22},{16,24},... | collective-permute-start | bytes 153608 | tf_op jit(solution)/shard_map/ppermute | solution.py:155
  389.5 90.2 %collective-permute-start.65 = (bf16[512,640]{1,0:T(8,128)(2,1)}, bf16[512,640]{1,0:T(8,128)(2,1)}, u32[]{:S(2)}, u32[]{:S(2)}) collective-permute-start(bf16[512,640]{1,0:T(8,128)(2,1)} %get-tuple-element.112), channel_id=1, source_target_pairs={{0,1},{1,0},{2,3},{3,2},{4,5},{5,4},{6,7},{7,6},{8,9},{9,8},{10,11... | collective-permute-start | bytes 1966088 | tf_op jit(solution)/shard_map/ppermute | solution.py:113
  395.3 31.7 %collective-permute-start.17 = (bf16[4,2,80,960]{3,2,0,1:T(8,128)(2,1)S(1)}, bf16[4,2,80,960]{3,2,0,1:T(8,128)(2,1)}, u32[]{:S(2)}, u32[]{:S(2)}) collective-permute-start(bf16[4,2,80,960]{3,2,0,1:T(8,128)(2,1)S(1)} %bitcast.412), channel_id=1, source_target_pairs={{0,4},{2,6},{4,0},{6,2},{8,12},{10,14},{12,8},{14,10},{16,20},{18,... | collective-permute-start | bytes 3686408 | tf_op jit(solution)/shard_map/ppermute | solution.py:118
  398.1 32.6 %collective-permute-start.9 = (bf16[4,2,80,960]{3,2,0,1:T(8,128)(2,1)S(1)}, bf16[4,2,80,960]{3,2,0,1:T(8,128)(2,1)}, u32[]{:S(2)}, u32[]{:S(2)}) collective-permute-start(bf16[4,2,80,960]{3,2,0,1:T(8,128)(2,1)S(1)} %bitcast.411), channel_id=1, source_target_pairs={{0,2},{2,0},{4,6},{6,4},{8,10},{10,8},{12,14},{14,12},{16,18},{18,... | collective-permute-start | bytes 3686408 | tf_op jit(solution)/shard_map/ppermute | solution.py:118
  410.9 99.5 %collective-permute-start.55 = (bf16[4,2,80,1280]{3,2,0,1:T(8,128)(2,1)}, bf16[4,2,80,1280]{3,2,0,1:T(8,128)(2,1)S(1)}, u32[]{:S(2)}, u32[]{:S(2)}) collective-permute-start(bf16[4,2,80,1280]{3,2,0,1:T(8,128)(2,1)} %bitcast.388), channel_id=1, source_target_pairs={{0,4},{2,6},{4,0},{6,2},{8,12},{10,14},{12,8},{14,10},{16,20},{18,... | collective-permute-start | bytes 4915208 | tf_op jit(solution)/shard_map/ppermute | solution.py:118
  428.9 15.9 %collective-permute-start.18 = (bf16[4,80,960]{2,1,0:T(8,128)(2,1)S(1)}, bf16[4,80,960]{2,1,0:T(8,128)(2,1)S(1)}, u32[]{:S(2)}, u32[]{:S(2)}) collective-permute-start(bf16[4,80,960]{2,1,0:T(8,128)(2,1)S(1)} %dynamic-slice_bitcast_fusion.4), channel_id=1, source_target_pairs={{0,2},{2,0},{4,6},{6,4},{8,10},{10,8},{12,14},{14,12},{16,18},{18,... | collective-permute-start | bytes 1843208 | tf_op jit(solution)/shard_map/ppermute | solution.py:118
  432.6 42.9 %collective-permute-start.10 = (bf16[4,80,960]{2,1,0:T(8,128)(2,1)S(1)}, bf16[4,80,960]{2,1,0:T(8,128)(2,1)S(1)}, u32[]{:S(2)}, u32[]{:S(2)}) collective-permute-start(bf16[4,80,960]{2,1,0:T(8,128)(2,1)S(1)} %dynamic-slice_bitcast_fusion.5), channel_id=1, source_target_pairs={{0,4},{2,6},{4,0},{6,2},{8,12},{10,14},{12,8},{14,10},{16,20},{18,... | collective-permute-start | bytes 1843208 | tf_op jit(solution)/shard_map/ppermute | solution.py:118
  444.8 94.6 %collective-permute-start.47 = (bf16[4,2,80,1280]{3,2,0,1:T(8,128)(2,1)S(1)}, bf16[4,2,80,1280]{3,2,0,1:T(8,128)(2,1)S(1)}, u32[]{:S(2)}, u32[]{:S(2)}) collective-permute-start(bf16[4,2,80,1280]{3,2,0,1:T(8,128)(2,1)S(1)} %bitcast.410), channel_id=1, source_target_pairs={{0,2},{2,0},{4,6},{6,4},{8,10},{10,8},{12,14},{14,12},{16,18},{18,... | collective-permute-start | bytes 4915208 | tf_op jit(solution)/shard_map/ppermute | solution.py:118
  475.6 21.6 %collective-permute-start.19 = (bf16[80,960]{1,0:T(8,128)(2,1)S(1)}, bf16[80,960]{1,0:T(8,128)(2,1)S(1)}, u32[]{:S(2)}, u32[]{:S(2)}) collective-permute-start(bf16[80,960]{1,0:T(8,128)(2,1)S(1)} %get-tuple-element.145), channel_id=1, source_target_pairs={{0,8},{2,10},{4,12},{6,14},{1,9},{3,11},{5,13},{7,15}} | collective-permute-start | bytes 460808 | tf_op jit(solution)/shard_map/ppermute | solution.py:155
  479.7 19.6 %collective-permute-start.22 = (bf16[80,960]{1,0:T(8,128)(2,1)S(1)}, bf16[80,960]{1,0:T(8,128)(2,1)S(1)}, u32[]{:S(2)}, u32[]{:S(2)}) collective-permute-start(bf16[80,960]{1,0:T(8,128)(2,1)S(1)} %get-tuple-element.146), channel_id=1, source_target_pairs={{24,16},{26,18},{28,20},{30,22},{25,17},{27,19},{29,21},{31,23}} | collective-permute-start | bytes 460808 | tf_op jit(solution)/shard_map/ppermute | solution.py:156
  480.4 17.5 %collective-permute-start.11 = (bf16[80,960]{1,0:T(8,128)(2,1)S(1)}, bf16[80,960]{1,0:T(8,128)(2,1)S(1)}, u32[]{:S(2)}, u32[]{:S(2)}) collective-permute-start(bf16[80,960]{1,0:T(8,128)(2,1)S(1)} %get-tuple-element.149), channel_id=1, source_target_pairs={{0,8},{2,10},{4,12},{6,14},{1,9},{3,11},{5,13},{7,15}} | collective-permute-start | bytes 460808 | tf_op jit(solution)/shard_map/ppermute | solution.py:155
  499.3 92.2 %collective-permute-start.74 = (bf16[4,2,320,320]{3,2,0,1:T(8,128)(2,1)S(1)}, bf16[4,2,320,320]{3,2,0,1:T(8,128)(2,1)S(1)}, u32[]{:S(2)}, u32[]{:S(2)}) collective-permute-start(bf16[4,2,320,320]{3,2,0,1:T(8,128)(2,1)S(1)} %bitcast.409), channel_id=1, source_target_pairs={{0,4},{2,6},{4,0},{6,2},{8,12},{10,14},{12,8},{14,10},{16,20},{18,... | collective-permute-start | bytes 4915208 | tf_op jit(solution)/shard_map/ppermute | solution.py:118
  507.0 103.2 %collective-permute-start.66 = (bf16[4,2,320,320]{3,2,0,1:T(8,128)(2,1)S(1)}, bf16[4,2,320,320]{3,2,0,1:T(8,128)(2,1)S(1)}, u32[]{:S(2)}, u32[]{:S(2)}) collective-permute-start(bf16[4,2,320,320]{3,2,0,1:T(8,128)(2,1)S(1)} %bitcast.408), channel_id=1, source_target_pairs={{0,2},{2,0},{4,6},{6,4},{8,10},{10,8},{12,14},{14,12},{16,18},{18,... | collective-permute-start | bytes 4915208 | tf_op jit(solution)/shard_map/ppermute | solution.py:118
  533.3 34.5 %collective-permute-start.56 = (bf16[4,80,1280]{2,1,0:T(8,128)(2,1)S(1)}, bf16[4,80,1280]{2,1,0:T(8,128)(2,1)S(1)}, u32[]{:S(2)}, u32[]{:S(2)}) collective-permute-start(bf16[4,80,1280]{2,1,0:T(8,128)(2,1)S(1)} %dynamic-slice_bitcast_fusion.2), channel_id=1, source_target_pairs={{0,2},{2,0},{4,6},{6,4},{8,10},{10,8},{12,14},{14,12},{16,18},{18,... | collective-permute-start | bytes 2457608 | tf_op jit(solution)/shard_map/ppermute | solution.py:118
  539.8 31.2 %collective-permute-start.48 = (bf16[4,80,1280]{2,1,0:T(8,128)(2,1)S(1)}, bf16[4,80,1280]{2,1,0:T(8,128)(2,1)S(1)}, u32[]{:S(2)}, u32[]{:S(2)}) collective-permute-start(bf16[4,80,1280]{2,1,0:T(8,128)(2,1)S(1)} %dynamic-slice_bitcast_fusion.3), channel_id=1, source_target_pairs={{0,4},{2,6},{4,0},{6,2},{8,12},{10,14},{12,8},{14,10},{16,20},{18,... | collective-permute-start | bytes 2457608 | tf_op jit(solution)/shard_map/ppermute | solution.py:118
  591.5 16.3 %collective-permute-start.51 = (bf16[80,1280]{1,0:T(8,128)(2,1)S(1)}, bf16[80,1280]{1,0:T(8,128)(2,1)S(1)}, u32[]{:S(2)}, u32[]{:S(2)}) collective-permute-start(bf16[80,1280]{1,0:T(8,128)(2,1)S(1)} %get-tuple-element.139), channel_id=1, source_target_pairs={{0,8},{2,10},{4,12},{6,14},{8,16},{10,18},{12,20},{14,22},{16,24},... | collective-permute-start | bytes 614408 | tf_op jit(solution)/shard_map/ppermute | solution.py:155
  597.7 18.3 %collective-permute-start.75 = (bf16[4,320,320]{2,1,0:T(8,128)(2,1)S(1)}, bf16[4,320,320]{2,1,0:T(8,128)(2,1)S(1)}, u32[]{:S(2)}, u32[]{:S(2)}) collective-permute-start(bf16[4,320,320]{2,1,0:T(8,128)(2,1)S(1)} %dynamic-slice_bitcast_fusion), channel_id=1, source_target_pairs={{0,2},{2,0},{4,6},{6,4},{8,10},{10,8},{12,14},{14,12},{16,18},{18,... | collective-permute-start | bytes 2457608 | tf_op jit(solution)/shard_map/ppermute | solution.py:118
  610.9 24.2 %collective-permute-start.67 = (bf16[4,320,320]{2,1,0:T(8,128)(2,1)S(1)}, bf16[4,320,320]{2,1,0:T(8,128)(2,1)S(1)}, u32[]{:S(2)}, u32[]{:S(2)}) collective-permute-start(bf16[4,320,320]{2,1,0:T(8,128)(2,1)S(1)} %dynamic-slice_bitcast_fusion.1), channel_id=1, source_target_pairs={{0,4},{2,6},{4,0},{6,2},{8,12},{10,14},{12,8},{14,10},{16,20},{18,... | collective-permute-start | bytes 2457608 | tf_op jit(solution)/shard_map/ppermute | solution.py:118
  616.3 23.8 %collective-permute-start.76 = (bf16[320,320]{1,0:T(8,128)(2,1)S(1)}, bf16[320,320]{1,0:T(8,128)(2,1)S(1)}, u32[]{:S(2)}, u32[]{:S(2)}) collective-permute-start(bf16[320,320]{1,0:T(8,128)(2,1)S(1)} %get-tuple-element.123), channel_id=1, source_target_pairs={{0,8},{2,10},{4,12},{6,14},{1,9},{3,11},{5,13},{7,15}} | collective-permute-start | bytes 614408 | tf_op jit(solution)/shard_map/ppermute | solution.py:155
  620.6 29.6 %collective-permute-start.79 = (bf16[320,320]{1,0:T(8,128)(2,1)S(1)}, bf16[320,320]{1,0:T(8,128)(2,1)S(1)}, u32[]{:S(2)}, u32[]{:S(2)}) collective-permute-start(bf16[320,320]{1,0:T(8,128)(2,1)S(1)} %get-tuple-element.124), channel_id=1, source_target_pairs={{24,16},{26,18},{28,20},{30,22},{25,17},{27,19},{29,21},{31,23}} | collective-permute-start | bytes 614408 | tf_op jit(solution)/shard_map/ppermute | solution.py:156
  639.4 17.4 %collective-permute-start.71 = (bf16[320,320]{1,0:T(8,128)(2,1)S(1)}, bf16[320,320]{1,0:T(8,128)(2,1)S(1)}, u32[]{:S(2)}, u32[]{:S(2)}) collective-permute-start(bf16[320,320]{1,0:T(8,128)(2,1)S(1)} %get-tuple-element.128), channel_id=1, source_target_pairs={{24,16},{26,18},{28,20},{30,22},{25,17},{27,19},{29,21},{31,23}} | collective-permute-start | bytes 614408 | tf_op jit(solution)/shard_map/ppermute | solution.py:156
  (133 other events, 1191.6 us)

commit v2 on v0

--- a/solution.py
+++ b/solution.py
@@ -1,12 +1,16 @@
+import functools
 import math
 
 import jax
 import jax.numpy as jnp
 from jax import lax
+from jax.experimental import pallas as pl
+from jax.experimental.pallas import tpu as pltpu
 from jax.sharding import PartitionSpec as P
 
 HEADS = 16
-
+F32 = jnp.float32
+BF16 = jnp.bfloat16
 
 epsilon = 1e-06
 
@@ -106,6 +110,546 @@
     return lax.dot_general(
         left, right, (((1,), (1,)), ((), ())), preferred_element_type=jnp.float32
     )
+
+
+def swap_cores(values):
+    return lax.ppermute(values, "head", [(0, 1), (1, 0)])
+
+
+def flip(values, bit):
+    size = lax.axis_size("dp")
+    return lax.ppermute(values, "dp", [(i, i ^ bit) for i in range(size)])
+
+
+def scatter_rows(left, right):
+    return lax.psum_scatter(
+        contract_rows(left, right), ("dp", "head"), scatter_dimension=0, tiled=True
+    )
+
+
+def sum_everywhere(values, over_head):
+    size = lax.axis_size("dp")
+    if over_head:
+        values = values + swap_cores(values)
+    bit = 1
+    while bit < size:
+        values = values + flip(values, bit)
+        bit *= 2
+    return values
+
+
+MESH = pl.DeviceIdType.MESH
+
+
+def chunk_table(width, hidden):
+    half = width // 2
+    table = [(0, 0)]
+    table += [(1, j) for j in range(hidden // width)]
+    table += [(2, j) for j in range(hidden // width)]
+    table += [(3, 0)]
+    table += [(4, j) for j in range(3)]
+    return table, half
+
+
+def gradient_kernel(
+    table,
+    size,
+    block,
+    cols,
+    y_t,
+    g_t,
+    a2_t,
+    o_t,
+    a1_t,
+    cot,
+    e3,
+    eh,
+    e2,
+    ep,
+    small,
+    out_head,
+    out_down,
+    out_up,
+    out_out,
+    out_qkv,
+    out_small,
+    y_o,
+    g_o,
+    a2_o,
+    o_o,
+    a1_o,
+    e3_o,
+    eh_o,
+    e2_o,
+    ep_o,
+    lbuf,
+    rbuf,
+    grad,
+    recv1,
+    pair,
+    recv2,
+    line,
+    recv_up,
+    recv_down,
+    total,
+    sums,
+    sums_in,
+    push_send,
+    push_recv,
+    load_sem,
+    send1_sem,
+    recv1_sem,
+    send2_sem,
+    recv2_sem,
+    up_send,
+    up_recv,
+    down_send,
+    down_recv,
+    local_sem,
+    swap_send,
+    swap_recv,
+    small_send,
+    small_recv,
+):
+    n = len(table)
+    length = size // 4
+    me = lax.axis_index("dp")
+    core = lax.axis_index("head")
+    xi = lax.rem(me, 2)
+    yi = lax.rem(me // 2, 2)
+    zi = me // 4
+    tokens = e3.shape[0]
+    flip_x = me + 1 - 2 * xi
+    flip_y = me + 2 * (1 - 2 * yi)
+    first_bit = jnp.where(core == 0, xi, yi)
+    second_bit = jnp.where(core == 0, yi, xi)
+    first_peer = jnp.where(core == 0, flip_x, flip_y)
+    second_peer = jnp.where(core == 0, flip_y, flip_x)
+    other = 1 - core
+    far = lax.rem(me + size // 2, size)
+    zbit = lax.rem(zi, 2)
+    near = me + 4 * (1 - 2 * zbit)
+
+    barrier = pltpu.get_barrier_semaphore()
+    for index, which in ((me, other), (flip_x, core), (flip_y, core), (far, core)):
+        pl.semaphore_signal(barrier, inc=1, device_id=(index, which), device_id_type=MESH)
+
+    @pl.when(zi > 0)
+    def _():
+        pl.semaphore_signal(barrier, inc=1, device_id=(me - 4, core), device_id_type=MESH)
+
+    @pl.when(zi < length - 1)
+    def _():
+        pl.semaphore_signal(barrier, inc=1, device_id=(me + 4, core), device_id_type=MESH)
+
+    inner = jnp.where(zi > 0, 1, 0) + jnp.where(zi < length - 1, 1, 0)
+    pl.semaphore_wait(barrier, 4 + inner)
+
+    def remote(src, dst, send, recv, index, which):
+        return pltpu.make_async_remote_copy(
+            src_ref=src,
+            dst_ref=dst,
+            send_sem=send,
+            recv_sem=recv,
+            device_id=(index, which),
+            device_id_type=MESH,
+        )
+
+    lefts = (y_t, g_t, a2_t, o_t, a1_t)
+    left_others = (y_o, g_o, a2_o, o_o, a1_o)
+    rights = (cot, e3, eh, e2, ep)
+    right_others = (None, e3_o, eh_o, e2_o, ep_o)
+
+    def push_left(i):
+        return remote(
+            lefts[i], left_others[i], push_send.at[i], push_recv.at[i], me, other
+        )
+
+    def push_right(i):
+        wide = rights[i].shape[1] // 2
+        start = pl.multiple_of(other * wide, 128)
+        return remote(
+            rights[i].at[:, pl.ds(start, wide)],
+            right_others[i],
+            push_send.at[4 + i],
+            push_recv.at[4 + i],
+            me,
+            other,
+        )
+
+    for i in range(5):
+        if i > 0:
+            push_right(i).start()
+        push_left(i).start()
+
+    def loads(i, j, slot):
+        lower = pl.ds(j * block, block) if i == 1 else slice(None)
+        copies = []
+        for half, source in ((0, lefts[i]), (1, left_others[i])):
+            copies.append((source.at[:, lower, :], lbuf.at[slot, half], load_sem.at[slot, half]))
+        if i == 0:
+            mine = pl.multiple_of(core * tokens, 16)
+            its = pl.multiple_of(other * tokens, 16)
+            copies.append((cot.at[pl.ds(mine, tokens)], rbuf.at[slot, 0], load_sem.at[slot, 2]))
+            copies.append((cot.at[pl.ds(its, tokens)], rbuf.at[slot, 1], load_sem.at[slot, 3]))
+        else:
+            wide = rights[i].shape[1] // 2
+            shift = 0 if i == 1 else j * cols
+            start = pl.multiple_of(core * wide + shift, 128)
+            copies.append(
+                (rights[i].at[:, pl.ds(start, cols)], rbuf.at[slot, 0], load_sem.at[slot, 2])
+            )
+            copies.append(
+                (
+                    right_others[i].at[:, pl.ds(shift, cols)],
+                    rbuf.at[slot, 1],
+                    load_sem.at[slot, 3],
+                )
+            )
+        return copies
+
+    def start_load(c, slot):
+        i, j = table[c]
+        if j == 0:
+            push_left(i).wait_recv()
+            if i > 0:
+                push_right(i).wait_recv()
+        for copy in loads(i, j, slot):
+            pltpu.make_async_copy(*copy).start()
+
+    start_load(0, 0)
+    start_load(1, 1)
+
+    peers = ((me, other), (flip_x, core), (flip_y, core), (near, core), (far, core))
+    steps = len(peers)
+
+    def small_copy(i):
+        return remote(
+            sums.at[i], sums_in.at[i], small_send.at[i], small_recv.at[i], peers[i][0], peers[i][1]
+        )
+
+    sums[0] = small[...]
+    small_copy(0).start()
+
+    def send1(slot, c):
+        return remote(
+            grad.at[slot, 1 - first_bit],
+            recv1.at[c],
+            send1_sem.at[slot],
+            recv1_sem.at[c],
+            first_peer,
+            core,
+        )
+
+    def send2(slot, c):
+        return remote(
+            pair.at[slot, 1 - second_bit],
+            recv2.at[c],
+            send2_sem.at[slot],
+            recv2_sem.at[c],
+            second_peer,
+            core,
+        )
+
+    def send_up(slot, c, step):
+        return remote(
+            line.at[slot, jnp.minimum(zi + (length - step), length - 1)],
+            recv_up.at[c, step - 1],
+            up_send.at[slot, step - 1],
+            up_recv.at[c, step - 1],
+            jnp.minimum(me + 4, size - 1),
+            core,
+        )
+
+    def send_down(slot, c, step):
+        return remote(
+            line.at[slot, jnp.maximum(zi - (length - step), 0)],
+            recv_down.at[c, step - 1],
+            down_send.at[slot, step - 1],
+            down_recv.at[c, step - 1],
+            jnp.maximum(me - 4, 0),
+            core,
+        )
+
+    def start_line(slot, c, step):
+        @pl.when(zi < step)
+        def _():
+            send_up(slot, c, step).start()
+
+        @pl.when(zi >= length - step)
+        def _():
+            send_down(slot, c, step).start()
+
+    def wait_line_sent(slot, c, step):
+        @pl.when(zi < step)
+        def _():
+            send_up(slot, c, step).wait_send()
+
+        @pl.when(zi >= length - step)
+        def _():
+            send_down(slot, c, step).wait_send()
+
+    def results(c):
+        i, j = table[c]
+        if i == 0:
+            return [(None, pltpu.make_async_copy(total.at[c], out_head, local_sem.at[c]))]
+        if i == 1:
+            owner = j // 2
+            target = out_down.at[
+                pl.ds((j % 2) * block, block), pl.ds(pl.multiple_of(core * cols, 128), cols)
+            ]
+            return [
+                (core == owner, pltpu.make_async_copy(total.at[c], target, local_sem.at[c])),
+                (
+                    core != owner,
+                    remote(total.at[c], target, swap_send.at[c], swap_recv.at[c], me, other),
+                ),
+            ]
+        target = (None, None, out_up, out_out, out_qkv)[i]
+        wide = target.shape[1] // 2
+        place = target.at[:, pl.ds(pl.multiple_of(core * wide + j * cols, 128), cols)]
+        half = block // 2
+        mine = pl.ds(pl.multiple_of(core * half, 8), half)
+        its = pl.ds(pl.multiple_of(other * half, 8), half)
+        return [
+            (None, pltpu.make_async_copy(total.at[c, mine], place, local_sem.at[c])),
+            (None, remote(total.at[c, its], place, swap_send.at[c], swap_recv.at[c], me, other)),
+        ]
+
+    def guarded(condition, action):
+        if condition is None:
+            action()
+        else:
+            pl.when(condition)(action)
+
+    @pl.loop(0, n + 2 + length)
+    def _(t):
+        slot = lax.rem(t, 2)
+
+        @pl.when(t < n)
+        def _():
+            @pl.when(t >= 2)
+            def _():
+                send1(slot, t - 2).wait_send()
+
+            for half in range(2):
+                pltpu.make_async_copy(
+                    lbuf.at[slot, half], lbuf.at[slot, half], load_sem.at[slot, half]
+                ).wait()
+                pltpu.make_async_copy(
+                    rbuf.at[slot, half], rbuf.at[slot, half], load_sem.at[slot, 2 + half]
+                ).wait()
+
+            @pl.loop(0, length)
+            def _(z):
+                rows = pl.ds(z * 4, 4)
+                value = None
+                for half in range(2):
+                    left = lbuf[slot, half, rows].reshape(4 * block, tokens)
+                    part = jnp.dot(left, rbuf[slot, half], preferred_element_type=F32)
+                    value = part if value is None else value + part
+                value = value.astype(BF16)
+                for q in range(4):
+                    x, y = q % 2, q // 2
+                    one = jnp.where(core == 0, x, y)
+                    two = jnp.where(core == 0, y, x)
+                    grad[slot, one, two, z] = value[q * block : (q + 1) * block]
+
+            send1(slot, t).start()
+
+            for c in range(2, n):
+
+                @pl.when(t == c - 2)
+                def _():
+                    start_load(c, c % 2)
+
+        @pl.when((t >= 1) & (t <= n))
+        def _():
+            c = t - 1
+            spot = lax.rem(c, 2)
+            send1(spot, c).wait_recv()
+
+            @pl.when(c >= 2)
+            def _():
+                send2(spot, c - 2).wait_send()
+
+            for two in range(2):
+
+                @pl.loop(0, length)
+                def _(z):
+                    pair[spot, two, z] = (
+                        grad[spot, first_bit, two, z].astype(F32) + recv1[c, two, z].astype(F32)
+                    ).astype(BF16)
+
+            send2(spot, c).start()
+
+        @pl.when((t >= 2) & (t <= n + 1))
+        def _():
+            c = t - 2
+            spot = lax.rem(c, 2)
+            ring = lax.rem(c, length + 1)
+            send2(spot, c).wait_recv()
+
+            @pl.loop(0, length)
+            def _(z):
+                line[ring, z] = (
+                    pair[spot, second_bit, z].astype(F32) + recv2[c, z].astype(F32)
+                ).astype(BF16)
+
+            start_line(ring, c, 1)
+
+        for step in range(1, length):
+
+            @pl.when((t >= 2 + step) & (t <= n + 1 + step))
+            def _():
+                c = t - 2 - step
+                ring = lax.rem(c, length + 1)
+                last = step == length - 1
+
+                up_in = (zi >= 1) & (zi <= step)
+                down_in = (zi <= length - 2) & (zi >= length - 1 - step)
+
+                @pl.when(up_in)
+                def _():
+                    send_up(ring, c, step).wait_recv()
+                    spot = jnp.minimum(zi + (length - 1 - step), length - 1)
+                    if not last:
+                        line[ring, spot] = (
+                            line[ring, spot].astype(F32) + recv_up[c, step - 1].astype(F32)
+                        ).astype(BF16)
+
+                @pl.when(down_in)
+                def _():
+                    send_down(ring, c, step).wait_recv()
+                    spot = jnp.maximum(zi - (length - 1 - step), 0)
+                    if not last:
+                        line[ring, spot] = (
+                            line[ring, spot].astype(F32) + recv_down[c, step - 1].astype(F32)
+                        ).astype(BF16)
+
+                if not last:
+                    start_line(ring, c, step + 1)
+                else:
+                    total[c] = line[ring, zi].astype(F32)
+
+                    @pl.when(up_in)
+                    def _():
+                        total[c] = total[c] + recv_up[c, step - 1].astype(F32)
+
+                    @pl.when(down_in)
+                    def _():
+                        total[c] = total[c] + recv_down[c, step - 1].astype(F32)
+
+                    for back in range(1, length):
+                        wait_line_sent(ring, c, back)
+
+                    for d in range(n):
+
+                        @pl.when(c == d)
+                        def _():
+                            for condition, copy in results(d):
+                                guarded(condition, copy.start)
+
+        for i in range(steps):
+
+            @pl.when(t == i + 1)
+            def _():
+                small_copy(i).wait()
+                value = sums[i] + sums_in[i]
+                if i == steps - 1:
+                    out_small[...] = value
+                else:
+                    sums[i + 1] = value
+                    small_copy(i + 1).start()
+
+    for c in range(n):
+        i, j = table[c]
+        copies = results(c)
+        if i == 0:
+            copies[0][1].wait()
+        elif i == 1:
+            (here, local), (away, sent) = copies
+            guarded(here, local.wait)
+            guarded(away, sent.wait_send)
+            guarded(here, sent.wait_recv)
+        else:
+            copies[0][1].wait()
+            copies[1][1].wait()
+    for slot in ((n - 2) % 2, (n - 1) % 2):
+        send1(slot, 0).wait_send()
+        send2(slot, 0).wait_send()
+    for i in range(5):
+        push_left(i).wait_send()
+        if i > 0:
+            push_right(i).wait_send()
+
+
+def reduce_gradients(lefts, rights, small):
+    size = lax.axis_size("dp")
+    width, tokens = lefts[0].shape
+    hidden = lefts[1].shape[0]
+    block = width // size
+    table, cols = chunk_table(width, hidden)
+    n = len(table)
+    length = size // 4
+    share = block // 2
+    hbm = pl.BlockSpec(memory_space=pl.ANY)
+    vmem = pl.BlockSpec(memory_space=pltpu.VMEM)
+    lefts = [left.reshape(size, left.shape[0] // size, tokens) for left in lefts]
+    shapes = [
+        jax.ShapeDtypeStruct((block, cols), F32),
+        jax.ShapeDtypeStruct((hidden // size // 2, width), F32),
+        jax.ShapeDtypeStruct((share, hidden), F32),
+        jax.ShapeDtypeStruct((share, width), F32),
+        jax.ShapeDtypeStruct((share, 3 * width), F32),
+        jax.ShapeDtypeStruct(small.shape, F32),
+    ]
+    shapes += [jax.ShapeDtypeStruct(left.shape, BF16) for left in lefts]
+    shapes += [
+        jax.ShapeDtypeStruct((tokens, right.shape[1] // 2), BF16) for right in rights[1:]
+    ]
+    dma = pltpu.SemaphoreType.DMA
+    results = pl.pallas_call(
+        functools.partial(gradient_kernel, table, size, block, cols),
+        out_shape=shapes,
+        in_specs=[hbm] * 10 + [vmem],
+        out_specs=[hbm] * 5 + [vmem] + [hbm] * 9,
+        scratch_shapes=[
+            pltpu.VMEM((2, 2, size, block, tokens), BF16),
+            pltpu.VMEM((2, 2, tokens, cols), BF16),
+            pltpu.VMEM((2, 2, 2, length, block, cols), BF16),
+            pltpu.VMEM((n, 2, length, block, cols), BF16),
+            pltpu.VMEM((2, 2, length, block, cols), BF16),
+            pltpu.VMEM((n, length, block, cols), BF16),
+            pltpu.VMEM((length + 1, length, block, cols), BF16),
+            pltpu.VMEM((n, length - 1, block, cols), BF16),
+            pltpu.VMEM((n, length - 1, block, cols), BF16),
+            pltpu.VMEM((n, block, cols), F32),
+            pltpu.VMEM((5,) + small.shape, F32),
+            pltpu.VMEM((5,) + small.shape, F32),
+            dma((9,)),
+            dma((9,)),
+            dma((2, 4)),
+            dma((2,)),
+            dma((n,)),
+            dma((2,)),
+            dma((n,)),
+            dma((length + 1, length - 1)),
+            dma((n, length - 1)),
+            dma((length + 1, length - 1)),
+            dma((n, length - 1)),
+            dma((n,)),
+            dma((n,)),
+            dma((n,)),
+            dma((5,)),
+            dma((5,)),
+        ],
+        compiler_params=pltpu.CompilerParams(
+            collective_id=0, has_side_effects=True, vmem_limit_bytes=60 << 20
+        ),
+        name="gradients",
+    )(*lefts, *rights, small)
+    return results[:6]
 
 
 def per_device(
@@ -122,10 +666,19 @@
     head_output_bias,
     cotangent,
 ):
+    core = lax.axis_index("head")
+    place = lax.axis_index("dp")
     rows, sequence_span = segment_ids.shape
-    width = inputs.shape[1]
+    count, width = inputs.shape
     hdim = width // HEADS
     scale = 1.0 / math.sqrt(hdim)
+
+    other_rows = lax.dynamic_slice_in_dim(cotangent, (1 - core) * count, count, 0)
+    own_rows = lax.dynamic_slice_in_dim(cotangent, core * count, count, 0)
+    got = swap_cores(contract_cols(other_rows, head_projection_weight).astype(BF16))
+    grad_final = contract_cols(own_rows, head_projection_weight) + got.astype(F32)
+    bias_local = jnp.sum(cotangent, axis=0, dtype=F32)
+
     cosine, sine = rotary_tables(sequence_span, hdim)
     tokens = inputs.astype(jnp.float32)
     normed_one, inverse_one = rms_forward(tokens, gain_attn)
@@ -148,40 +701,28 @@
     resid_three = resid_two + jnp.dot(hidden, w_down, preferred_element_type=jnp.float32)
     normed_three, inverse_three = rms_forward(resid_three, gain_final)
     final_hidden = normed_three.astype(jnp.bfloat16)
-    collected_rows = lax.all_gather(final_hidden, "head", axis=0, tiled=True)
+    other_hidden = swap_cores(final_hidden)
+    collected_rows = jnp.concatenate(
+        [
+            jnp.where(core == 0, final_hidden, other_hidden),
+            jnp.where(core == 0, other_hidden, final_hidden),
+        ],
+        axis=0,
+    )
     predicted_levels = (
         jnp.dot(collected_rows, head_projection_weight, preferred_element_type=jnp.float32)
         + head_output_bias
     )
-    grad_final = lax.psum_scatter(
-        contract_cols(cotangent, head_projection_weight).astype(jnp.bfloat16),
-        "head",
-        scatter_dimension=0,
-        tiled=True,
-    ).astype(jnp.float32)
-    head_local = contract_rows(collected_rows, cotangent)
-    bias_local = jnp.sum(cotangent, axis=0, dtype=jnp.float32)
-    grad_head = lax.psum_scatter(head_local, "dp", scatter_dimension=0, tiled=True)
-    grad_bias = lax.psum(bias_local, "dp")
     grad_three, grad_gain_final = rms_backward(resid_three, inverse_three, gain_final, grad_final)
     grad_mlp_out = grad_three.astype(jnp.bfloat16)
-    grad_down = contract_rows(hidden, grad_mlp_out)
     grad_hidden = contract_cols(grad_mlp_out, w_down)
     sigmoid = jax.nn.sigmoid(hidden_pre)
     grad_pre = (grad_hidden * sigmoid * (1.0 + hidden_pre * (1.0 - sigmoid))).astype(jnp.bfloat16)
-    grad_up = contract_rows(act_two, grad_pre)
     grad_norm_two, grad_gain_mlp = rms_backward(
         resid_two, inverse_two, gain_mlp, contract_cols(grad_pre, w_up)
     )
     grad_two = grad_three + grad_norm_two
-    mlp_sums = (
-        lax.psum_scatter(grad_up, ("dp", "head"), scatter_dimension=0, tiled=True),
-        lax.psum_scatter(grad_down, ("dp", "head"), scatter_dimension=0, tiled=True),
-        lax.psum_scatter(grad_gain_mlp, ("dp", "head"), scatter_dimension=0, tiled=True),
-        lax.psum_scatter(grad_gain_final, ("dp", "head"), scatter_dimension=0, tiled=True),
-    )
     grad_branch = grad_two.astype(jnp.bfloat16)
-    grad_out = contract_rows(mixed, grad_branch)
     grad_mixed = (
         contract_cols(grad_branch, w_out)
         .astype(jnp.bfloat16)
@@ -198,28 +739,49 @@
         .reshape(rows * sequence_span, 3 * width)
         .astype(jnp.bfloat16)
     )
-    grad_qkv = contract_rows(act_one, grad_proj)
     grad_norm_one, grad_gain_attn = rms_backward(
         tokens, inverse_one, gain_attn, contract_cols(grad_proj, w_qkv)
     )
     entry_sensitivity_matrix = grad_two + grad_norm_one
-    attn_sums = (
-        lax.psum_scatter(grad_qkv, ("dp", "head"), scatter_dimension=0, tiled=True),
-        lax.psum_scatter(grad_out, ("dp", "head"), scatter_dimension=0, tiled=True),
-        lax.psum_scatter(grad_gain_attn, ("dp", "head"), scatter_dimension=0, tiled=True),
-    )
-    sum_up, sum_down, sum_gain_mlp, sum_gain_final = mlp_sums
-    sum_qkv, sum_out, sum_gain_attn = attn_sums
+    size = lax.axis_size("dp")
+    share = width // (2 * size)
+    if size == 16 and lax.axis_size("head") == 2:
+        half = width // 2
+        bias_row = lax.dynamic_update_slice_in_dim(
+            jnp.zeros((width,), F32), bias_local, core * half, 0
+        )
+        blank = jnp.zeros((width,), F32)
+        small = jnp.stack(
+            [grad_gain_attn, grad_gain_mlp, grad_gain_final, bias_row] + [blank] * 4
+        )
+        grad_head, grad_down, grad_up, grad_out, grad_qkv, sums = reduce_gradients(
+            [final_hidden.T, hidden.T, act_two.T, mixed.T, act_one.T],
+            [cotangent, grad_mlp_out, grad_pre, grad_branch, grad_proj],
+            small,
+        )
+        gains = lax.dynamic_slice_in_dim(sums, (place * 2 + core) * share, share, 1)
+        grad_bias = lax.dynamic_slice_in_dim(sums[3], core * half, half, 0)
+    else:
+        grad_head = lax.psum_scatter(
+            contract_rows(collected_rows, cotangent), "dp", scatter_dimension=0, tiled=True
+        )
+        grad_down = scatter_rows(hidden, grad_mlp_out)
+        grad_up = scatter_rows(act_two, grad_pre)
+        grad_out = scatter_rows(mixed, grad_branch)
+        grad_qkv = scatter_rows(act_one, grad_proj)
+        gains = sum_everywhere(jnp.stack([grad_gain_attn, grad_gain_mlp, grad_gain_final]), True)
+        gains = lax.dynamic_slice_in_dim(gains, (place * 2 + core) * share, share, 1)
+        grad_bias = sum_everywhere(bias_local, False)
     return (
         predicted_levels,
         entry_sensitivity_matrix,
-        sum_gain_attn,
-        sum_qkv,
-        sum_out,
-        sum_gain_mlp,
-        sum_up,
-        sum_down,
-        sum_gain_final,
+        gains[0],
+        grad_qkv,
+        grad_out,
+        gains[1],
+        grad_up,
+        grad_down,
+        gains[2],
         grad_head,
         grad_bias,
     )

time: 1180 us -> 459 us (0.39)
  waiting for transfers between devices: 823 us -> 0.01 us
  Pallas kernels: 0 us -> 216 us
  blocking collectives: 81.4 us -> 0 us
  matrix products: 191 us -> 143 us
  local copies, waits for them, and re-layouts: 14.4 us -> 39.8 us
  between operations: 15.1 us -> 1.74 us
    reduce_scatter x6 -> x0, waiting for transfers between devices: 809 us -> none  [the longest x1 288 us: per_device(): lax.psum_scatter(grad_up, ('dp', 'head'), scatter_dimension=0, tiled=True)]
    pallas_call x0 -> x1, Pallas kernels: none -> 216 us  [reduce_gradients(): pl.pallas_call(functools.partial(gradient_kernel, table, size, block, col...]
    dot_general x5 -> x0, matrix products: 53.6 us -> none  [contract_rows(): lax.dot_general(left, right, (((0,), (0,)), ((), ())), preferred_element_...]
    psum x1 -> x0, blocking collectives: 42.9 us -> none  [per_device(): grad_bias = lax.psum(bias_local, 'dp')]
    unnamed x1 -> x0, blocking collectives: 38.6 us -> none
    convert_element_type x0 -> x2, local copies, waits for them, and re-layouts: none -> 14.4 us  [the longest x1 8.1 us: per_device(): hidden = jax.nn.silu(hidden_pre).astype(jnp.bfloat16)]
    all_gather x1 -> x0, waiting for transfers between devices: 14.2 us -> none  [per_device(): collected_rows = lax.all_gather(final_hidden, 'head', axis=0, tiled=True)]
    dot_general x5 -> x6, matrix products: 53.9 us -> 54.4 us  [contract_cols(): lax.dot_general(left, right, (((1,), (1,)), ((), ())), preferred_element_...]
  transfers between devices with their start and end apart: 7 -> 2, of which waited for: 5 -> 0; matrix products, arithmetic and copies ran while one was open for 16% -> 21% of each run, Pallas kernels for 0% -> 48%
where the time goes in v2:
time: 459 us; the launch traced here: 450 us
  Pallas kernels  216 us (47%)
  matrix products  143 us (31%)
  other arithmetic  48.9 us (11%)
  local copies, waits for them, and re-layouts  39.8 us (9%)
    pallas_call x1, Pallas kernels, reduce_gradients(): pl.pallas_call(functools.partial(gradient_kernel, table, size, block, col...  216 us
    dot_general x6, matrix products, contract_cols(): lax.dot_general(left, right, (((1,), (1,)), ((), ())), preferred_element_...  54.4 us
    dot_general x1, matrix products, per_device(): hidden_pre = jnp.dot(act_two, w_up, preferred_element_type=jnp.float32)  16.4 us
    dot_general x1, matrix products, attend_backward(): jnp.einsum('qhd,khd->hqk', grad_attended, value, preferred_element_type=j...  15.7 us
    dot_general x1, matrix products, per_device(): jnp.dot(hidden, w_down, preferred_element_type=jnp.float32)  13 us
    convert_element_type x1, other arithmetic, attend_backward(): grad_scores = (probs * (grad_probs - jnp.sum(grad_probs * probs, axis=-1,...  12.7 us
    unnamed x109, local copies, waits for them, and re-layouts  11.4 us
    reduce_sum x1, other arithmetic, attend_forward(): overall_number = jnp.sum(expo, axis=-1, keepdims=True)  9.8 us
  transfers between devices with their start and end apart: 2, of which 0 were waited for; matrix products, arithmetic and copies ran while one was open for 21% of the time, Pallas kernels for 48%

profile of v2, /device:TPU:0, one launch (start us, length us, event | category | flops | bytes accessed | tf_op | source)
XLA Modules:
  0.0 450.0 jit_solution(12198303939840119584)
XLA Ops:
  0.7 4.1 convolution_convert_fusion
  5.6 8.3 %fusion.50 = f32[512,3840]{0,1:T(8,128)S(1)} fusion(bf16[1280,3840]{1,0:T(8,128)(2,1)} %param.15, bf16[512,1280]{1,0:T(8,128)(2,1)S(1)} %copy-done.6, f32[1280]{0:T(1024)S(1)} %copy-done.36, f32[512]{0:T(512)S(1)} %add_rsqrt_fusion.2), kind=kOutput, calls=%fused_computation.91 | convolution fusion | flops 5035786240 | bytes 19012608 | tf_op jit(solution)/shard_map/dot_general | solution.py:686
  14.9 2.4 copy-done.13
  18.9 8.0 %fusion.1 = (f32[16,512]{1,0:T(8,128)}, f32[16,512,512]{1,2,0:T(8,128)}) fusion(pred[512,512]{0,1:T(8,128)(4,1)S(1)} %fusion.37, bf16[512,16,40]{0,2,1:T(8,128)(2,1)S(1)} %get-tuple-element.99, bf16[512,16,40]{0,2,1:T(8,128)(2,1)S(1)} %get-tuple-element.100, bf16[512,16,40]{0,2,1:T(8,128)(2,1)S(1)} %get-tuple-element.89, ...), kind=kOutput, calls=%fused_computation.7 | convolution fusion | flops 688906240 | bytes 19693568 | tf_op jit(solution)/shard_map/while/body/eval_jaxpr/qhd,khd->hqk/dot_general | solution.py:62
  26.9 9.8 %fusion = f32[16,512]{1,0:T(8,128)} fusion(f32[16,512,512]{1,2,0:T(8,128)} %get-tuple-element.107, f32[16,512]{1,0:T(8,128)} %get-tuple-element.106, pred[512,512]{0,1:T(8,128)(4,1)S(1)} %fusion.37), kind=kLoop, calls=%fused_computation.6 | loop fusion | flops 16769024 | bytes 17104896 | tf_op jit(solution)/shard_map/while/body/eval_jaxpr/reduce_sum | solution.py:72
  36.7 9.2 %fusion.32.o_t = bf16[16,80,512]{2,1,0:T(8,128)(2,1)S(1)} fusion(f32[16,512,512]{1,2,0:T(8,128)} %get-tuple-element.107, f32[16,512]{1,0:T(8,128)} %fusion, f32[16,512]{1,0:T(8,128)} %get-tuple-element.106, pred[512,512]{0,1:T(8,128)(4,1)S(1)} %fusion.37, f32[1,512,3,16,80]{1,4,3,2,0:T(8,128)} %bitcast.102), kind=kOutput, calls=%fused_computation.62 | convolution fusion | flops 692715520 | bytes 19726336 | tf_op jit(solution)/shard_map/while/body/eval_jaxpr/hqk,khd->qhd/dot_general | solution.py:74
  46.0 2.2 multiply_reduce_fusion.6
  48.2 16.4 %fusion.5 = (bf16[5120,512]{0,1:T(8,128)(2,1)}, f32[512,5120]{1,0:T(8,128)}) fusion(bf16[1280,5120]{1,0:T(8,128)(2,1)} %param.18, f32[512,1280]{1,0:T(8,128)S(1)} %get-tuple-element.109, f32[1280]{0:T(1024)S(1)} %copy-done.35, f32[512]{0:T(512)S(1)} %add_rsqrt_fusion.1), kind=kOutput, calls=%fused_computation.16 | convolution fusion | flops 6725959680 | bytes 31464448 | tf_op jit(solution)/shard_map/dot_general | solution.py:699
  64.7 13.0 %multiply_reduce_fusion.5 = (f32[512]{0:T(512)}, f32[512,1280]{1,0:T(8,128)}) fusion(f32[512,1280]{1,0:T(8,128)S(1)} %get-tuple-element.109, bf16[5120,1280]{1,0:T(8,128)(2,1)S(1)} %bitcast.108, f32[512,5120]{1,0:T(8,128)} %get-tuple-element.116), kind=kOutput, calls=%fused_computation.57 | convolution fusion | flops 6725959168 | bytes 28837888 | tf_op jit(solution)/shard_map/dot_general | solution.py:701
  77.7 8.1 %copy.44 = bf16[5120,512]{1,0:T(8,128)(2,1)} copy(bf16[5120,512]{0,1:T(8,128)(2,1)} %get-tuple-element.115) | data formatting | bytes 10485760 | tf_op jit(solution)/shard_map/convert_element_type | solution.py:700
  89.5 5.1 %multiply_reduce_fusion.1 = (f32[1280]{0:T(1024)}, f32[512]{0:T(512)S(1)}, f32[512,1280]{1,0:T(8,128)S(1)}) fusion(f32[512,1280]{1,0:T(8,128)} %get-tuple-element.111, f32[512]{0:T(512)S(1)} %add_rsqrt_fusion, bf16[512,1280]{1,0:T(8,128)(2,1)} %collective-permute-done.1, f32[1280]{0:T(1024)S(1)} %copy-done.34, bf16[1280,640]{1,0:T(8,128)(2,1)} %param.21, ...), kind=kOutput, calls=%fused_computation.47 | convolution fusion | flops 844101888 | bytes 8861700 | tf_op jit(solution)/shard_map/dot_general | solution.py:110
  96.2 2.0 fusion.68.e3
  98.3 21.2 %multiply_convert_fusion.1.eh = bf16[512,5120]{1,0:T(8,128)(2,1)} fusion(f32[512,5120]{1,0:T(8,128)} %get-tuple-element.116, bf16[512,1280]{1,0:T(8,128)(2,1)S(1)} %fusion.68.e3, bf16[5120,1280]{1,0:T(8,128)(2,1)} %param.19), kind=kOutput, calls=%fused_computation.13 | convolution fusion | flops 6734479360 | bytes 30146560 | tf_op jit(solution)/shard_map/dot_general | solution.py:110
  119.5 11.6 %fusion.70 = f32[512,1280]{1,0:T(8,128)S(1)} fusion(bf16[512,5120]{1,0:T(8,128)(2,1)} %multiply_convert_fusion.1.eh, bf16[1280,5120]{1,0:T(8,128)(2,1)} %param.18), kind=kOutput, calls=%fused_computation.125 | convolution fusion | flops 6710886400 | bytes 20971520 | tf_op jit(solution)/shard_map/dot_general | solution.py:110
  131.2 2.4 multiply_reduce_fusion.2
  133.6 4.1 fusion.69
  138.8 3.0 convolution_convert_fusion.1
  141.7 2.4 copy.39
  144.2 15.7 %multiply_reduce_fusion = (f32[16,512]{1,0:T(8,128)S(1)}, f32[16,512,512]{1,2,0:T(8,128)}) fusion(f32[16,512]{1,0:T(8,128)} %log_add_fusion, f32[16,512,512]{1,2,0:T(8,128)} %get-tuple-element.107, pred[512,512]{0,1:T(8,128)(4,1)S(1)} %fusion.37, bf16[512,16,80]{0,2,1:T(8,128)(2,1)} %bitcast.104, f32[1,512,3,16,80]{1,4,3,2,0:T(8,128)} %bitcast.103), kind=kOutput, calls=%fused_computation.1 | convolution fusion | flops 696246272 | bytes 36503552 | tf_op jit(solution)/shard_map/while/body/eval_jaxpr/qhd,khd->hqk/dot_general | solution.py:88
  159.8 12.7 %multiply_convert_fusion = bf16[16,512,512]{1,2,0:T(8,128)(2,1)S(1)} fusion(f32[16,512,512]{1,2,0:T(8,128)} %get-tuple-element.114, f32[16,512]{1,0:T(8,128)S(1)} %get-tuple-element.113, f32[16,512]{1,0:T(8,128)S(1)} %copy-done.33, f32[16,512,512]{1,2,0:T(8,128)} %get-tuple-element.107, pred[512,512]{0,1:T(8,128)(4,1)S(1)} %fusion.37), kind=kLoop, calls=%fused_computation | loop fusion | flops 29360128 | bytes 42270720 | tf_op jit(solution)/shard_map/while/body/eval_jaxpr/convert_element_type | solution.py:93
  172.6 2.6 multiply_bitcast_fusion
  176.6 8.3 %fusion.33 = bf16[1,512,1,16,80]{1,4,3,2,0:T(8,128)(2,1)S(1)} fusion(bf16[512,16,80]{0,2,1:T(8,128)(2,1)S(1)} %bitcast.105, f32[16,512]{1,0:T(8,128)S(1)} %copy-done.33, f32[16,512,512]{1,2,0:T(8,128)} %get-tuple-element.107, pred[512,512]{0,1:T(8,128)(4,1)S(1)} %fusion.37), kind=kOutput, calls=%fused_computation.63 | convolution fusion | flops 692715520 | bytes 19693568 | tf_op jit(solution)/shard_map/while/body/eval_jaxpr/hqk,qhd->khd/dot_general | solution.py:82
  186.6 1.9 copy-done.8
  188.4 9.4 %fusion.71 = f32[512,1280]{1,0:T(8,128)} fusion(bf16[512,3840]{0,1:T(8,128)(2,1)S(1)} %bitcast.94, bf16[1280,3840]{1,0:T(8,128)(2,1)} %param.15), kind=kOutput, calls=%fused_computation.126 | convolution fusion | flops 5033164800 | bytes 16384000 | tf_op jit(solution)/shard_map/dot_general | solution.py:110
  197.9 6.3 %copy.47.ep = bf16[512,3840]{1,0:T(8,128)(2,1)} copy(bf16[512,3840]{0,1:T(8,128)(2,1)} %bitcast.95) | data formatting | bytes 7864320 | tf_op jit(solution)/shard_map/convert_element_type | solution.py:740
  204.1 4.0 fusion.20
  208.2 2.4 copy.46
  210.7 2.4 copy.43
  213.2 2.4 copy.45
  216.3 215.9 %gradients.1 = (f32[80,640]{1,0:T(8,128)}, f32[160,1280]{1,0:T(8,128)}, f32[40,5120]{1,0:T(8,128)}, f32[40,1280]{1,0:T(8,128)}, f32[40,3840]{1,0:T(8,128)}, /*in...) custom-call(bf16[16,80,512]{2,1,0:T(8,128)(2,1)} %bitcast.99, ...), custom_call_target="tpu_custom_call" | custom-call | tf_op jit(solution)/shard_map/gradients/pallas_call | solution.py:612
  434.8 5.2 %fusion.19 = f32[512,1280]{1,0:T(8,128)} fusion(f32[512,1280]{1,0:T(8,128)} %get-tuple-element.81, bf16[512,1280]{1,0:T(8,128)(2,1)} %param.12, f32[512,1280]{1,0:T(8,128)} %fusion.71, f32[512]{0:T(512)S(1)} %broadcast_multiply_fusion, f32[1280]{0:T(1024)S(1)} %copy-done.37, f32[512]{0:T(512)S(1)} %copy-done.43), kind=kLoop, calls=%fused_computation.36 | loop fusion | flops 4587520 | bytes 9184256 | tf_op jit(solution)/shard_map/add | solution.py:745
  441.9 3.7 fusion.26
  (142 shorter events, 21.8 us)
Async XLA Ops:
  0.6 45.3 %copy-start = (bf16[1280,1280]{1,0:T(8,128)(2,1)S(1)}, bf16[1280,1280]{1,0:T(8,128)(2,1)}, u32[]{:S(2)}) copy-start(bf16[1280,1280]{1,0:T(8,128)(2,1)} %param.16) | copy-start | bytes 9830404
  0.7 4.9 %copy-start.36 = (f32[1280]{0:T(1024)S(1)}, f32[1280]{0:T(1024)}, u32[]{:S(2)}) copy-start(f32[1280]{0:T(1024)} %param.14) | copy-start | bytes 15364
  4.7 84.8 %collective-permute-start.1 = (bf16[512,1280]{1,0:T(8,128)(2,1)}, bf16[512,1280]{1,0:T(8,128)(2,1)}, u32[]{:S(2)}, u32[]{:S(2)}) collective-permute-start(bf16[512,1280]{1,0:T(8,128)(2,1)} %convolution_convert_fusion), channel_id=1, source_target_pairs={{0,1},{1,0},{2,3},{3,2},{4,5},{5,4},{6,7},{7,6},{8,9},{9,8},{10,11... | collective-permute-start | bytes 3932168 | tf_op jit(solution)/shard_map/ppermute | solution.py:116
  5.6 8.4 %copy-start.42 = (f32[512]{0:T(512)}, f32[512]{0:T(512)S(1)}, u32[]{:S(2)}) copy-start(f32[512]{0:T(512)S(1)} %add_rsqrt_fusion.2) | copy-start | bytes 6148
  18.8 8.1 %copy-start.14 = (bf16[512,16,40]{0,2,1:T(8,128)(2,1)}, bf16[512,16,40]{0,2,1:T(8,128)(2,1)S(1)}, u32[]{:S(2)}) copy-start(bf16[512,16,40]{0,2,1:T(8,128)(2,1)S(1)} %get-tuple-element.99) | copy-start | bytes 1966084
  18.8 8.0 %copy-start.16 = (bf16[512,16,40]{0,2,1:T(8,128)(2,1)}, bf16[512,16,40]{0,2,1:T(8,128)(2,1)S(1)}, u32[]{:S(2)}) copy-start(bf16[512,16,40]{0,2,1:T(8,128)(2,1)S(1)} %get-tuple-element.100) | copy-start | bytes 1966084
  18.8 8.0 %copy-start.18 = (bf16[512,16,40]{0,2,1:T(8,128)(2,1)}, bf16[512,16,40]{0,2,1:T(8,128)(2,1)S(1)}, u32[]{:S(2)}) copy-start(bf16[512,16,40]{0,2,1:T(8,128)(2,1)S(1)} %get-tuple-element.88) | copy-start | bytes 1966084
  18.9 8.0 %copy-start.20 = (bf16[512,16,40]{0,2,1:T(8,128)(2,1)}, bf16[512,16,40]{0,2,1:T(8,128)(2,1)S(1)}, u32[]{:S(2)}) copy-start(bf16[512,16,40]{0,2,1:T(8,128)(2,1)S(1)} %get-tuple-element.89) | copy-start | bytes 1966084
  36.7 9.3 %copy-start.7 = (bf16[512,1280]{1,0:T(8,128)(2,1)S(1)}, bf16[512,1280]{1,0:T(8,128)(2,1)}, u32[]{:S(2)}) copy-start(bf16[512,1280]{1,0:T(8,128)(2,1)} %param.12) | copy-start | bytes 3932164
  46.0 18.7 %slice-start = ((s8[13107200]{0:T(1024)(128)(4,1)}), s8[4194304]{0:T(1024)(128)(4,1)S(1)}, s32[]{:S(2)}) async-start(s8[13107200]{0:T(1024)(128)(4,1)} %bitcast.107), calls=%async_computation | async-start | bytes 8388608
  48.1 16.5 %copy-start.1 = (f32[512,1280]{1,0:T(8,128)}, f32[512,1280]{1,0:T(8,128)S(1)}, u32[]{:S(2)}) copy-start(f32[512,1280]{1,0:T(8,128)S(1)} %get-tuple-element.109) | copy-start | bytes 7864324
  48.1 16.5 %copy-start.44 = (f32[512]{0:T(512)}, f32[512]{0:T(512)S(1)}, u32[]{:S(2)}) copy-start(f32[512]{0:T(512)S(1)} %add_rsqrt_fusion.1) | copy-start | bytes 6148
  48.2 16.5 %slice-start.1 = ((s8[13107200]{0:T(1024)(128)(4,1)}), s8[4194304]{0:T(1024)(128)(4,1)S(1)}, s32[]{:S(2)}) async-start(s8[13107200]{0:T(1024)(128)(4,1)} %bitcast.107), calls=%async_computation.1 | async-start | bytes 8388608
  48.2 16.5 %slice-start.2 = ((s8[13107200]{0:T(1024)(128)(4,1)}), s8[4194304]{0:T(1024)(128)(4,1)S(1)}, s32[]{:S(2)}) async-start(s8[13107200]{0:T(1024)(128)(4,1)} %bitcast.107), calls=%async_computation.2 | async-start | bytes 8388608
  48.2 16.5 %slice-start.3 = ((s8[13107200]{0:T(1024)(128)(4,1)}), s8[524288]{0:T(1024)(128)(4,1)S(1)}, s32[]{:S(2)}) async-start(s8[13107200]{0:T(1024)(128)(4,1)} %bitcast.107), calls=%async_computation.3 | async-start | bytes 1048576
  77.7 11.8 %copy-start.34 = (f32[1280]{0:T(1024)S(1)}, f32[1280]{0:T(1024)}, u32[]{:S(2)}) copy-start(f32[1280]{0:T(1024)} %param.20) | copy-start | bytes 15364
  89.5 6.7 %copy-start.3 = (f32[512,1280]{1,0:T(8,128)S(1)}, f32[512,1280]{1,0:T(8,128)}, u32[]{:S(2)}) copy-start(f32[512,1280]{1,0:T(8,128)} %get-tuple-element.111) | copy-start | bytes 7864324
  98.2 21.2 %copy-start.12 = (bf16[512,1280]{1,0:T(8,128)(2,1)}, bf16[512,1280]{1,0:T(8,128)(2,1)S(1)}, u32[]{:S(2)}) copy-start(bf16[512,1280]{1,0:T(8,128)(2,1)S(1)} %fusion.68.e3) | copy-start | bytes 3932164
  119.5 11.7 %copy-start.2 = (f32[512,1280]{1,0:T(8,128)S(1)}, f32[512,1280]{1,0:T(8,128)}, u32[]{:S(2)}) copy-start(f32[512,1280]{1,0:T(8,128)} %copy-done.1) | copy-start | bytes 7864324
  119.5 11.7 %copy-start.45 = (f32[512]{0:T(512)S(1)}, f32[512]{0:T(512)}, u32[]{:S(2)}) copy-start(f32[512]{0:T(512)} %copy-done.44) | copy-start | bytes 6148
  144.1 15.7 %copy-start.33 = (f32[16,512]{1,0:T(8,128)S(1)}, f32[16,512]{1,0:T(8,128)}, u32[]{:S(2)}) copy-start(f32[16,512]{1,0:T(8,128)} %log_add_fusion) | copy-start | bytes 98308
  159.8 12.7 %copy-start.19 = (bf16[512,16,40]{0,2,1:T(8,128)(2,1)S(1)}, bf16[512,16,40]{0,2,1:T(8,128)(2,1)}, u32[]{:S(2)}) copy-start(bf16[512,16,40]{0,2,1:T(8,128)(2,1)} %copy-done.18) | copy-start | bytes 1966084
  159.8 12.8 %copy-start.21 = (bf16[512,16,40]{0,2,1:T(8,128)(2,1)S(1)}, bf16[512,16,40]{0,2,1:T(8,128)(2,1)}, u32[]{:S(2)}) copy-start(bf16[512,16,40]{0,2,1:T(8,128)(2,1)} %copy-done.20) | copy-start | bytes 1966084
  176.6 8.4 %copy-start.27 = (f32[512,40]{0,1:T(8,128)S(1)}, f32[512,40]{0,1:T(8,128)}, u32[]{:S(2)}) copy-start(f32[512,40]{0,1:T(8,128)} %copy-done.26) | copy-start | bytes 245764
  176.6 8.4 %copy-start.29 = (f32[512,40]{0,1:T(8,128)S(1)}, f32[512,40]{0,1:T(8,128)}, u32[]{:S(2)}) copy-start(f32[512,40]{0,1:T(8,128)} %copy-done.28) | copy-start | bytes 245764
  197.9 6.3 %copy-start.37 = (f32[1280]{0:T(1024)S(1)}, f32[1280]{0:T(1024)}, u32[]{:S(2)}) copy-start(f32[1280]{0:T(1024)} %param.14) | copy-start | bytes 15364
  197.9 6.3 %copy-start.43 = (f32[512]{0:T(512)S(1)}, f32[512]{0:T(512)}, u32[]{:S(2)}) copy-start(f32[512]{0:T(512)} %copy-done.42) | copy-start | bytes 6148
  210.6 229.4 %collective-permute-start = (bf16[512,1280]{1,0:T(8,128)(2,1)}, bf16[512,1280]{1,0:T(8,128)(2,1)}, u32[]{:S(2)}, u32[]{:S(2)}) collective-permute-start(bf16[512,1280]{1,0:T(8,128)(2,1)} %get-tuple-element.93), channel_id=1, source_target_pairs={{0,1},{1,0},{2,3},{3,2},{4,5},{5,4},{6,7},{7,6},{8,9},{9,8},{10,11... | collective-permute-start | bytes 3932168 | tf_op jit(solution)/shard_map/ppermute | solution.py:116
  210.7 4.9 %copy-start.41 = (f32[1,1280]{1,0:T(1,128)S(1)}, f32[1,1280]{1,0:T(1,128)}, u32[]{:S(2)}) copy-start(f32[1,1280]{1,0:T(1,128)} %copy-done.40) | copy-start | bytes 15364
  434.8 5.2 %copy-start.9 = (bf16[512,1280]{1,0:T(8,128)(2,1)S(1)}, bf16[512,1280]{1,0:T(8,128)(2,1)}, u32[]{:S(2)}) copy-start(bf16[512,1280]{1,0:T(8,128)(2,1)} %get-tuple-element.93) | copy-start | bytes 3932164
  441.9 4.5 %copy-start.32 = (f32[40,1280]{1,0:T(8,128)S(1)}, f32[40,1280]{1,0:T(8,128)}, u32[]{:S(2)}) copy-start(f32[40,1280]{1,0:T(8,128)} %get-tuple-element.134) | copy-start | bytes 614404
  441.9 5.2 %copy-start.25 = (f32[40,5120]{1,0:T(8,128)S(1)}, f32[40,5120]{1,0:T(8,128)}, u32[]{:S(2)}) copy-start(f32[40,5120]{1,0:T(8,128)} %get-tuple-element.136) | copy-start | bytes 2457604
  (22 other events, 55.3 us)
